TPU v7x, 32 devices: a whole 2x2x4 slice. The times are simulated.
32 devices in a mesh: gx: 8 (over z, x), gy: 4 (over y, core).
Axes of the slice: x: 2, y: 2, z: 4, core: 2. Of those that a mesh axis runs over, the one named last changes fastest.
Arguments:
- impedance: bfloat16 [8, 4, 1024, 1024], P('gx', 'gy'), may hold values from -0.1875 to 0.1875
- rebuild_map: bfloat16 [8, 4, 256, 1024], P('gx', 'gy'), may hold values from -0.1875 to 0.1875
- left_trace: bfloat16 [8, 4, 512, 512], P('gx', 'gy'), may hold values from -6 to 6
- lower_trace: bfloat16 [8, 4, 512, 512], P('gx', 'gy'), may hold values from -6 to 6
- cell_kind: int32 [128, 64], P('gx', 'gy'), may hold values from 0 to 15
- kind_wavenum: float32 [16], replicated, may hold values from 0.5 to 3
Outputs:
- right_trace: bfloat16 [8, 4, 512, 512], P('gx', 'gy')
- upper_trace: bfloat16 [8, 4, 512, 512], P('gx', 'gy')
- residual: float32 [128, 64, 512], P('gx', 'gy')
All inputs are finite; a program needn't handle non-finite values.
Results may differ from a plain program's by a relative error of at most 0.0064.
Values may be sent and summed in bfloat16 or wider, within the bound.
No kernel may reach another device: no remote copies, remote signals or barrier semaphores. Data moves between devices by JAX's collectives and lax.ppermute only.
A program may use at most 64 MiB of HBM per device.

v0:
```python
import functools

import jax
import jax.numpy as jnp
from jax import lax
from jax.experimental import pallas as pl
from jax.experimental.pallas import tpu as pltpu
from jax.sharding import PartitionSpec as P


STEPS = 4
CHUNKS = 2
F32 = jnp.float32
BF16 = jnp.bfloat16
VMEM = pl.BlockSpec(memory_space=pltpu.VMEM)
HBM = pl.BlockSpec(memory_space=pltpu.HBM)


def around(block, axis):
    count = lax.axis_size(axis)
    return lax.ppermute(block, axis, [(i, (i + 1) % count) for i in range(count)])


def onward(block, axis):
    count = lax.axis_size(axis)
    return lax.ppermute(block, axis, [(i, i + 1) for i in range(count - 1)])


def swapped(block, axis, first):
    names = ("gx", "gy")
    along = names.index(axis)
    sizes = tuple(lax.axis_size(name) for name in names)
    pairs = []
    for place in range(sizes[0] * sizes[1]):
        where = [place // sizes[1], place % sizes[1]]
        mate = first + ((where[along] - first) ^ 1)
        if 0 <= mate < sizes[along]:
            where[along] = mate
        elif axis == "gy":
            where[along] = sizes[along] - 1 - where[along]
        else:
            where[1 - along] ^= 1
        pairs.append((place, where[0] * sizes[1] + where[1]))
    return lax.ppermute(block, names, pairs)


def is_last(axis):
    return lax.axis_index(axis) == lax.axis_size(axis) - 1


PARAMS = pltpu.CompilerParams(vmem_limit_bytes=6 * 2**20)
PACKED = pltpu.CompilerParams(vmem_limit_bytes=6 * 2**20)


def cost(flops, moved):
    return pl.CostEstimate(flops=int(flops), bytes_accessed=int(moved), transcendentals=0)


def product(weights, left, lower):
    total, start = None, 0
    for piece in (*left, lower):
        rows = piece.shape[0]
        share = jnp.dot(weights[:, start : start + rows], piece[...], preferred_element_type=F32)
        total = share if total is None else total + share
        start += rows
    return total


def first_right_kernel(base, width, z_hbm, left_hbm, lower_hbm, out, z_top, left, lower, sem):
    rows = z_top.shape[0]
    split = rows * 6 // 8
    blocks = (pl.ds(0, split), pl.ds(split, rows - split))
    loads = [
        pltpu.make_async_copy(left_hbm.at[:, pl.ds(base, width)], left, sem.at[0]),
        pltpu.make_async_copy(lower_hbm.at[:, pl.ds(base, width)], lower, sem.at[1]),
    ]
    parts = [pltpu.make_async_copy(z_hbm.at[here], z_top.at[here], sem.at[2 + r]) for r, here in enumerate(blocks)]
    for copy in loads + parts:
        copy.start()
    for copy in loads:
        copy.wait()
    at_end = is_last("gx")
    for copy, here in zip(parts, blocks):
        copy.wait()
        out[here] = jnp.where(at_end, 0.0, product(z_top.at[here], [left], lower)).astype(BF16)


def first_right(z, left, lower, base, width):
    trace = left.shape[0]
    vmem = lambda *shape: jax.ShapeDtypeStruct(shape, BF16)
    return pl.pallas_call(
        functools.partial(first_right_kernel, base, width),
        out_shape=(vmem(trace, width), vmem(trace, 2 * trace), vmem(trace, width), vmem(trace, width)),
        in_specs=[HBM, HBM, HBM],
        out_specs=(VMEM,) * 4,
        scratch_shapes=[pltpu.SemaphoreType.DMA((4,))],
        cost_estimate=cost(4 * trace * trace * width, 4 * trace * trace + 6 * trace * width),
        compiler_params=PARAMS,
        name="first_right",
    )(z, left, lower)


def first_upper_kernel(z_hbm, left, lower, out, z_low, sem):
    rows = z_low.shape[0]
    block = rows // 2
    parts = [
        pltpu.make_async_copy(z_hbm.at[pl.ds(rows + r * block, block)], z_low.at[pl.ds(r * block, block)], sem.at[r])
        for r in range(2)
    ]
    for copy in parts:
        copy.start()
    at_end = is_last("gy")
    for r in range(2):
        parts[r].wait()
        here = pl.ds(r * block, block)
        out[here] = jnp.where(at_end, 0.0, product(z_low.at[here], [left], lower)).astype(BF16)


def first_upper(z, left, lower):
    trace, width = left.shape
    vmem = lambda *shape: jax.ShapeDtypeStruct(shape, BF16)
    return pl.pallas_call(
        first_upper_kernel,
        out_shape=(vmem(trace, width), vmem(trace, 2 * trace)),
        in_specs=[HBM, VMEM, VMEM],
        out_specs=(VMEM,) * 2,
        scratch_shapes=[pltpu.SemaphoreType.DMA((2,))],
        cost_estimate=cost(4 * trace * trace * width, 4 * trace * trace + 6 * trace * width),
        compiler_params=PARAMS,
        name="first_upper",
    )(z, left, lower)


def part_kernel(axis, z, left, lower, out):
    half = left.shape[0] // 2
    at_end = is_last(axis)
    for r in range(2):
        here = pl.ds(r * half, half)
        out[here] = jnp.where(at_end, 0.0, product(z.at[here], [left], lower)).astype(BF16)


def part(axis, z, left, lower):
    trace, width = left.shape
    return pl.pallas_call(
        functools.partial(part_kernel, axis),
        out_shape=jax.ShapeDtypeStruct((trace, width), BF16),
        in_specs=[VMEM] * 3,
        out_specs=VMEM,
        cost_estimate=cost(4 * trace * trace * width, 4 * trace * trace + 6 * trace * width),
        compiler_params=PARAMS,
        name="part",
    )(z, left, lower)


def part_loading_kernel(axis, base, z, left_hbm, lower_hbm, out, left, lower, sem):
    width = left.shape[1]
    loads = [
        pltpu.make_async_copy(left_hbm.at[:, pl.ds(base, width)], left, sem.at[0]),
        pltpu.make_async_copy(lower_hbm.at[:, pl.ds(base, width)], lower, sem.at[1]),
    ]
    for copy in loads:
        copy.start()
    for copy in loads:
        copy.wait()
    part_kernel(axis, z, left, lower, out)


def part_loading(axis, z, left, lower, base, width):
    trace = left.shape[0]
    block = jax.ShapeDtypeStruct((trace, width), BF16)
    return pl.pallas_call(
        functools.partial(part_loading_kernel, axis, base),
        out_shape=(block,) * 3,
        in_specs=[VMEM, HBM, HBM],
        out_specs=(VMEM,) * 3,
        scratch_shapes=[pltpu.SemaphoreType.DMA((2,))],
        cost_estimate=cost(4 * trace * trace * width, 4 * trace * trace + 6 * trace * width),
        compiler_params=PARAMS,
        name="part_loading",
    )(z, left, lower)


def wavenum_kernel(table, kinds, out):
    cells_x, cells_y = kinds.shape
    kind = kinds[...]
    value = jnp.zeros(kind.shape, F32)
    for k in range(table.shape[0]):
        value = jnp.where(kind == k, table[k], value)
    shape = (cells_y, cells_y)
    diagonal = lax.broadcasted_iota(jnp.int32, shape, 0) == lax.broadcasted_iota(jnp.int32, shape, 1)
    for x in range(cells_x):
        column = jnp.sum(jnp.where(diagonal, value[x : x + 1], 0.0), axis=1, keepdims=True)
        out[pl.ds(x * cells_y, cells_y)] = jnp.broadcast_to(column, (cells_y, out.shape[1]))


def wavenum_of(table, kinds):
    return pl.pallas_call(
        wavenum_kernel,
        out_shape=jax.ShapeDtypeStruct((kinds.size, 128), F32),
        in_specs=[pl.BlockSpec(memory_space=pltpu.SMEM), VMEM],
        out_specs=VMEM,
        compiler_params=PARAMS,
        name="wavenum",
    )(table, kinds)


def edge_rows(block, cells_y):
    cells = block.shape[0]
    row = lambda at, count: block[pl.ds(at, count)].astype(F32)
    return jnp.concatenate(
        [row(0, cells_y), row(cells - cells_y, cells_y)]
        + [row(x, 1) for x in range(0, cells, cells_y)]
        + [row(x + cells_y - 1, 1) for x in range(0, cells, cells_y)],
        axis=0,
    )


def volume_kernel(cells_y, weights, left, lower, volume, edges, edge_weights):
    volume[...] = product(weights, [left], lower)
    edges[...] = edge_rows(volume, cells_y).astype(BF16)
    edge_weights[...] = edge_rows(weights, cells_y).astype(BF16)


def volume_of(weights, left, lower, cells_y):
    width = left.shape[1]
    cells, depth = weights.shape
    lines = 2 * (cells_y + cells // cells_y)
    return pl.pallas_call(
        functools.partial(volume_kernel, cells_y),
        out_shape=(
            jax.ShapeDtypeStruct((cells, width), F32),
            jax.ShapeDtypeStruct((lines, width), BF16),
            jax.ShapeDtypeStruct((lines, depth), BF16),
        ),
        in_specs=[VMEM] * 3,
        out_specs=(VMEM,) * 3,
        cost_estimate=cost(2 * weights.size * width, 2 * weights.size + 4 * weights.shape[1] * width),
        compiler_params=PARAMS,
        name="volume",
    )(weights, left, lower)


def edges_kernel(weights, left, lower, done, x_pair, x_cross, y_pair, y_cross):
    old, width = done.shape[1], left.shape[1]
    fresh = product(weights, [left], lower).astype(BF16)
    even_x = lax.rem(lax.axis_index("gx"), 2) == 0
    even_y = lax.rem(lax.axis_index("gy"), 2) == 0
    deep, high = x_pair.shape[0], y_pair.shape[0]
    for where, block in ((pl.ds(0, old), done[...]), (pl.ds(old, width), fresh)):
        first, last = block[:deep], block[deep : 2 * deep]
        x_pair[:, where] = jnp.where(even_x, last, first)
        x_cross[:, where] = jnp.where(even_x, first, last)
        first, last = block[2 * deep : 2 * deep + high], block[2 * deep + high :]
        y_pair[:, where] = jnp.where(even_y, last, first)
        y_cross[:, where] = jnp.where(even_y, first, last)


def edges_of(weights, left, lower, done, cells_y):
    width = lower.shape[1]
    total = width + done.shape[1]
    line = lambda n: jax.ShapeDtypeStruct((n, total), BF16)
    cells_x = weights.shape[0] // 2 - cells_y
    return pl.pallas_call(
        edges_kernel,
        out_shape=(line(cells_y), line(cells_y), line(cells_x), line(cells_x)),
        in_specs=[VMEM] * 4,
        out_specs=(VMEM,) * 4,
        cost_estimate=cost(2 * weights.size * width, 2 * weights.size + 4 * weights.shape[1] * width),
        compiler_params=PARAMS,
        name="edges",
    )(weights, left, lower, done)


def last_kernel(z_top, z_low, left, lower, right_hbm, upper_hbm, right, upper, sem):
    width = left.shape[1]
    half = left.shape[0] // 2
    copies = []
    for z, out, out_hbm in ((z_top, right, right_hbm), (z_low, upper, upper_hbm)):
        for r in range(2):
            here = pl.ds(r * half, half)
            out[here] = product(z.at[here], [left], lower).astype(BF16)
            copies.append(
                pltpu.make_async_copy(out.at[here], out_hbm.at[here, pl.ds(0, width)], sem.at[len(copies)])
            )
            copies[-1].start()
    for copy in copies:
        copy.wait()


def last(z_top, z_low, left, lower, total):
    trace, width = left.shape
    out = jax.ShapeDtypeStruct((trace, total), BF16)
    return pl.pallas_call(
        last_kernel,
        out_shape=(out, out),
        in_specs=[VMEM] * 4,
        out_specs=(HBM, HBM),
        scratch_shapes=[
            pltpu.VMEM((trace, width), BF16),
            pltpu.VMEM((trace, width), BF16),
            pltpu.SemaphoreType.DMA((4,)),
        ],
        cost_estimate=cost(8 * trace * trace * width, 8 * trace * trace + 8 * trace * width),
        compiler_params=PARAMS,
        name="last",
    )(z_top, z_low, left, lower)


def plain_kernel(z_top, z_low, weights, left, lower, wavenum, first, *refs):
    right_hbm, inner, upper, right, second, sem = refs[-6:]
    left = [left]
    half, width = right.shape[0] // 2, right.shape[1]
    base = right_hbm.shape[1] - width
    copies = []
    for r in range(2):
        here = pl.ds(r * half, half)
        right[here] = product(z_top.at[here], left, lower).astype(BF16)
        copies.append(pltpu.make_async_copy(right.at[here], right_hbm.at[here, pl.ds(base, width)], sem.at[r]))
        copies[-1].start()
    for r in range(2):
        here = pl.ds(r * half, half)
        upper[here] = product(z_low.at[here], left, lower).astype(BF16)
    second[...] = product(weights, left, lower)
    cells_x, cells_y = inner.shape[:2]
    start = 0
    for volume in (first, second):
        where = pl.ds(start, volume.shape[1])
        start += volume.shape[1]
        place = lax.broadcasted_iota(jnp.int32, (cells_y, volume.shape[1]), 0)
        for x in range(cells_x):
            row = lambda k: volume[pl.ds(k * cells_y, cells_y)]
            here = row(x)
            around_it = jnp.where(place == 0, 0.0, pltpu.roll(here, 1, 0)) + jnp.where(
                place == cells_y - 1, 0.0, pltpu.roll(here, cells_y - 1, 0)
            )
            if x:
                around_it = around_it + row(x - 1)
            if x + 1 < cells_x:
                around_it = around_it + row(x + 1)
            scale = wavenum[pl.ds(x * cells_y, cells_y)][:, :1]
            inner[x, :, where] = around_it - 4.0 * here + scale * here
    for copy in copies:
        copy.wait()


def plain(z_top, z_low, weights, left, lower, wavenum, volume, before, cells_y):
    trace, width = lower.shape
    cells = volume.shape[0]
    total = before.shape[1]
    given = 7
    return pl.pallas_call(
        plain_kernel,
        out_shape=(
            jax.ShapeDtypeStruct(before.shape, before.dtype),
            jax.ShapeDtypeStruct((cells // cells_y, cells_y, total), F32),
            jax.ShapeDtypeStruct((trace, width), BF16),
        ),
        in_specs=[VMEM] * given + [HBM],
        out_specs=(HBM, VMEM, VMEM),
        scratch_shapes=[
            pltpu.VMEM((trace, width), BF16),
            pltpu.VMEM((cells, width), F32),
            pltpu.SemaphoreType.DMA((2,)),
        ],
        input_output_aliases={given: 0},
        cost_estimate=cost(8 * trace * trace * width, 8 * trace * trace + 8 * trace * width),
        compiler_params=PACKED,
        name="plain",
    )(z_top, z_low, weights, left, lower, wavenum, volume, before)


def beside(axis, pair, cross):
    place = lax.axis_index(axis)
    even = lax.rem(place, 2) == 0
    pair, cross = pair[...].astype(F32), cross[...].astype(F32)
    before = jnp.where(place == 0, 0.0, jnp.where(even, cross, pair))
    after = jnp.where(is_last(axis), 0.0, jnp.where(even, pair, cross))
    return before, after


def finish_kernel(inner, upper, x_pair, x_cross, y_pair, y_cross, _, upper_hbm, residual_hbm, out, sem):
    cells_x, cells_y, total = inner.shape
    groups = sem.shape[0] - 1
    deep = cells_x // groups
    before_x, after_x = beside("gx", x_pair, x_cross)
    before_y, after_y = beside("gy", y_pair, y_cross)
    place = lax.broadcasted_iota(jnp.int32, (cells_y, total), 0)
    width = upper.shape[1]
    base = upper_hbm.shape[1] - width
    copies = [pltpu.make_async_copy(upper, upper_hbm.at[:, pl.ds(base, width)], sem.at[groups])]
    copies[0].start()
    for group in range(groups):
        for x in range(group * deep, (group + 1) * deep):
            value = inner[x]
            value = value + jnp.where(
                place == 0, before_y[x : x + 1], jnp.where(place == cells_y - 1, after_y[x : x + 1], 0.0)
            )
            if x == 0:
                value = value + before_x
            if x == cells_x - 1:
                value = value + after_x
            out[x] = value
        here = pl.ds(group * deep, deep)
        copies.append(pltpu.make_async_copy(out.at[here], residual_hbm.at[here], sem.at[group]))
        copies[-1].start()
    for copy in copies:
        copy.wait()


def finish(inner, upper, halos, before):
    groups = 2 if inner.shape[0] % 2 == 0 else 1
    given = 2 + len(halos)
    return pl.pallas_call(
        finish_kernel,
        out_shape=(jax.ShapeDtypeStruct(before.shape, before.dtype), jax.ShapeDtypeStruct(inner.shape, F32)),
        in_specs=[VMEM] * given + [HBM],
        out_specs=(HBM, HBM),
        scratch_shapes=[pltpu.VMEM(inner.shape, F32), pltpu.SemaphoreType.DMA((groups + 1,))],
        input_output_aliases={given: 0},
        cost_estimate=cost(4 * inner.size, 8 * inner.size),
        compiler_params=PARAMS,
        name="finish",
    )(inner, upper, *halos, before)


def per_device(impedance, rebuild_map, left_trace, lower_trace, cell_kind, kind_wavenum):
    z = pltpu.with_memory_space_constraint(impedance[0, 0], pltpu.HBM)
    weights = rebuild_map[0, 0]
    left_all = pltpu.with_memory_space_constraint(left_trace[0, 0], pltpu.HBM)
    lower_all = pltpu.with_memory_space_constraint(lower_trace[0, 0], pltpu.HBM)
    sources = left_all.shape[1]
    width = sources // CHUNKS
    _, cells_y = cell_kind.shape
    left_in, lower_in = [None] * CHUNKS, [None] * CHUNKS
    for step in range(STEPS - 1):
        for c in range(CHUNKS):
            if step == 0 and c == 0:
                right, z_top, left, lower = first_right(z, left_all, lower_all, 0, width)
            elif step == 0:
                right, left, lower = part_loading("gx", z_top, left_all, lower_all, c * width, width)
            else:
                left, lower = left_in[c], lower_in[c]
                right = part("gx", z_top, left, lower)
            final = step == STEPS - 2 and c == CHUNKS - 1
            left_in[c] = onward(right, "gx") if final else around(right, "gx")
            if step == 0 and c == 0:
                upper, z_low = first_upper(z, left, lower)
            else:
                upper = part("gy", z_low, left, lower)
            lower_in[c] = around(upper, "gy")

    wavenum = wavenum_of(kind_wavenum, cell_kind)
    volume, edges, edge_weights = volume_of(weights, left_in[0], lower_in[0], cells_y)
    outs = last(z_top, z_low, left_in[0], lower_in[0], sources)
    volume, wavenum, left, lower, *outs = lax.optimization_barrier(
        (volume, wavenum, left_in[1], lower_in[1], *outs)
    )
    x_pair, x_cross, y_pair, y_cross = edges_of(edge_weights, left, lower, edges, cells_y)
    x_pair = swapped(x_pair, "gx", 0)
    x_cross = swapped(x_cross, "gx", 1)
    y_cross = swapped(y_cross, "gy", 1)
    y_pair = swapped(y_pair, "gy", 0)
    halos = (x_pair, x_cross, y_pair, y_cross)
    right_out, inner, upper = plain(z_top, z_low, weights, left, lower, wavenum, volume, outs[0], cells_y)
    upper_out, residual = finish(inner, upper, halos, outs[1])
    return (right_out[None, None], upper_out[None, None], residual)


def solution(mesh):
    return jax.shard_map(
        per_device,
        mesh=mesh,
        in_specs=(
            P("gx", "gy", None, None),
            P("gx", "gy", None, None),
            P("gx", "gy", None, None),
            P("gx", "gy", None, None),
            P("gx", "gy"),
            P(),
        ),
        out_specs=(P("gx", "gy", None, None), P("gx", "gy", None, None), P("gx", "gy", None)),
        check_vma=False,
    )
```

profile of v0, /device:TPU:0, one launch (start us, length us, event | category | flops | bytes accessed | tf_op | source)
XLA Modules:
  0.0 47.3 jit_solution(6802859988433265111)
XLA Ops:
  0.6 2.1 %first_right.1 = (bf16[512,256]{1,0:T(8,128)(2,1)S(1)}, bf16[512,1024]{1,0:T(8,128)(2,1)S(1)}, bf16[512,256]{1,0:T(8,128)(2,1)S(1)}, bf16[512,256]{1,0:T(8,128)(2,1)S(1)}) custom-call(bf16[1024,1024]{1,0:T(8,128)(2,1)} %bitcast.8, bf16[512,512]{1,0:T(8,128)(2,1)} %bitcast.10, bf16[512,512]{1,0:T(8,128)(2,1)} %bitcast.12), custom_call_target="tpu_custom_call" | custom-call | flops 268435456 | bytes 1835008 | tf_op jit(solution)/shard_map/first_right/pallas_call | solution.py:91
  2.7 3.0 %collective-permute-start = (bf16[512,256]{1,0:T(8,128)(2,1)S(1)}, bf16[512,256]{1,0:T(8,128)(2,1)S(1)}, u32[]{:S(2)}, u32[]{:S(2)}) collective-permute-start(bf16[512,256]{1,0:T(8,128)(2,1)S(1)} %get-tuple-element.36), channel_id=1, source_target_pairs={{0,4},{4,8},{8,12},{12,16},{16,20},{20,24},{24,28},{28,0},{1,5},{5... | collective-permute-start | bytes 786440 | tf_op jit(solution)/shard_map/ppermute | solution.py:21
  5.7 1.9 %first_upper.1 = (bf16[512,256]{1,0:T(8,128)(2,1)S(1)}, bf16[512,1024]{1,0:T(8,128)(2,1)S(1)}) custom-call(bf16[1024,1024]{1,0:T(8,128)(2,1)} %bitcast.9, bf16[512,256]{1,0:T(8,128)(2,1)S(1)} %get-tuple-element.33.left, bf16[512,256]{1,0:T(8,128)(2,1)S(1)} %get-tuple-element.34.lower), custom_call_target="tpu_custom_call" | custom-call | flops 268435456 | bytes 1835008 | tf_op jit(solution)/shard_map/first_upper/pallas_call | solution.py:122
  7.6 0.1 collective-permute-start.1
  7.7 1.5 %part_loading.1 = (bf16[512,256]{1,0:T(8,128)(2,1)S(1)}, bf16[512,256]{1,0:T(8,128)(2,1)S(1)}, bf16[512,256]{1,0:T(8,128)(2,1)S(1)}) custom-call(bf16[512,1024]{1,0:T(8,128)(2,1)S(1)} %get-tuple-element.32.z.z_top, bf16[512,512]{1,0:T(8,128)(2,1)} %bitcast.11, bf16[512,512]{1,0:T(8,128)(2,1)} %bitcast.13), custom_call_target="tpu_custom_call" | custom-call | flops 268435456 | bytes 1835008 | tf_op jit(solution)/shard_map/part_loading/pallas_call | solution.py:171
  9.2 1.6 %collective-permute-start.6 = (bf16[512,256]{1,0:T(8,128)(2,1)S(1)}, bf16[512,256]{1,0:T(8,128)(2,1)S(1)}, u32[]{:S(2)}, u32[]{:S(2)}) collective-permute-start(bf16[512,256]{1,0:T(8,128)(2,1)S(1)} %get-tuple-element.39), channel_id=1, source_target_pairs={{0,4},{4,8},{8,12},{12,16},{16,20},{20,24},{24,28},{28,0},{1,5},{5... | collective-permute-start | bytes 786440 | tf_op jit(solution)/shard_map/ppermute | solution.py:21
  10.8 0.4 part.13
  11.2 1.4 %collective-permute-start.7 = (bf16[512,256]{1,0:T(8,128)(2,1)S(1)}, bf16[512,256]{1,0:T(8,128)(2,1)S(1)}, u32[]{:S(2)}, u32[]{:S(2)}) collective-permute-start(bf16[512,256]{1,0:T(8,128)(2,1)S(1)} %part.13), channel_id=1, source_target_pairs={{0,1},{1,2},{2,3},{3,0},{4,5},{5,6},{6,7},{7,4},{8,9},{9,10},{10,1... | collective-permute-start | bytes 786440 | tf_op jit(solution)/shard_map/ppermute | solution.py:21
  12.6 2.4 %collective-permute-done.left = bf16[512,256]{1,0:T(8,128)(2,1)S(1)} collective-permute-done((bf16[512,256]{1,0:T(8,128)(2,1)S(1)}, bf16[512,256]{1,0:T(8,128)(2,1)S(1)}, u32[]{:S(2)}, u32[]{:S(2)}) %collective-permute-start) | collective-permute-done | bytes 262176 | tf_op jit(solution)/shard_map/ppermute | solution.py:21
  15.1 0.0 collective-permute-done.1.lower
  15.1 0.4 part.9
  15.5 0.1 collective-permute-start.2
  15.6 0.4 part.10
  16.0 0.1 collective-permute-start.3
  16.1 4.4 %collective-permute-done.6.left = bf16[512,256]{1,0:T(8,128)(2,1)S(1)} collective-permute-done((bf16[512,256]{1,0:T(8,128)(2,1)S(1)}, bf16[512,256]{1,0:T(8,128)(2,1)S(1)}, u32[]{:S(2)}, u32[]{:S(2)}) %collective-permute-start.6) | collective-permute-done | bytes 262176 | tf_op jit(solution)/shard_map/ppermute | solution.py:21
  20.5 0.0 collective-permute-done.7.lower
  20.5 0.4 part.14
  20.9 0.1 collective-permute-start.8
  21.0 0.4 part.15
  21.4 0.5 %collective-permute-start.9 = (bf16[512,256]{1,0:T(8,128)(2,1)S(1)}, bf16[512,256]{1,0:T(8,128)(2,1)S(1)}, u32[]{:S(2)}, u32[]{:S(2)}) collective-permute-start(bf16[512,256]{1,0:T(8,128)(2,1)S(1)} %part.15), channel_id=1, source_target_pairs={{0,1},{1,2},{2,3},{3,0},{4,5},{5,6},{6,7},{7,4},{8,9},{9,10},{10,1... | collective-permute-start | bytes 786440 | tf_op jit(solution)/shard_map/ppermute | solution.py:21
  21.9 4.8 %collective-permute-done.2.left = bf16[512,256]{1,0:T(8,128)(2,1)S(1)} collective-permute-done((bf16[512,256]{1,0:T(8,128)(2,1)S(1)}, bf16[512,256]{1,0:T(8,128)(2,1)S(1)}, u32[]{:S(2)}, u32[]{:S(2)}) %collective-permute-start.2) | collective-permute-done | bytes 262176 | tf_op jit(solution)/shard_map/ppermute | solution.py:21
  26.7 0.0 collective-permute-done.3.lower
  26.7 0.4 part.11
  27.2 0.1 collective-permute-start.4
  27.2 0.4 part.12
  27.7 0.0 copy-start.1
  27.7 0.0 copy-start.2
  27.7 0.0 copy-start
  27.7 0.1 collective-permute-start.5
  27.8 5.0 %collective-permute-done.8.left = bf16[512,256]{1,0:T(8,128)(2,1)S(1)} collective-permute-done((bf16[512,256]{1,0:T(8,128)(2,1)S(1)}, bf16[512,256]{1,0:T(8,128)(2,1)S(1)}, u32[]{:S(2)}, u32[]{:S(2)}) %collective-permute-start.8) | collective-permute-done | bytes 262176 | tf_op jit(solution)/shard_map/ppermute | solution.py:21
  32.8 0.0 collective-permute-done.9.lower
  32.8 0.4 part.16
  33.2 1.3 %collective-permute-start.10 = (bf16[512,256]{1,0:T(8,128)(2,1)S(1)}, bf16[512,256]{1,0:T(8,128)(2,1)S(1)}, u32[]{:S(2)}, u32[]{:S(2)}) collective-permute-start(bf16[512,256]{1,0:T(8,128)(2,1)S(1)} %part.16), channel_id=1, source_target_pairs={{0,4},{4,8},{8,12},{12,16},{16,20},{20,24},{24,28},{1,5},{5,9},{9,... | collective-permute-start | bytes 786440 | tf_op jit(solution)/shard_map/ppermute | solution.py:26
  34.5 0.4 part.17
  35.0 0.1 collective-permute-start.11
  35.0 0.0 copy-done.1
  35.0 0.0 copy-done.2
  35.1 0.7 %wavenum.1 = f32[256,128]{1,0:T(8,128)S(1)} custom-call(f32[16]{0:T(128)S(1)} %copy-done.2, s32[16,16]{1,0:T(8,128)S(1)} %copy-done.1), custom_call_target="tpu_custom_call" | custom-call | tf_op jit(solution)/shard_map/wavenum/pallas_call | solution.py:197
  35.7 2.3 %collective-permute-done.4.left = bf16[512,256]{1,0:T(8,128)(2,1)S(1)} collective-permute-done((bf16[512,256]{1,0:T(8,128)(2,1)S(1)}, bf16[512,256]{1,0:T(8,128)(2,1)S(1)}, u32[]{:S(2)}, u32[]{:S(2)}) %collective-permute-start.4) | collective-permute-done | bytes 262176 | tf_op jit(solution)/shard_map/ppermute | solution.py:21
  38.0 0.0 collective-permute-done.5.lower
  38.0 0.0 copy-done
  38.0 0.4 volume.1
  38.3 1.4 %last.1 = (bf16[512,512]{1,0:T(8,128)(2,1)}, bf16[512,512]{1,0:T(8,128)(2,1)}) custom-call(bf16[512,1024]{1,0:T(8,128)(2,1)S(1)} %get-tuple-element.32.z.z_top, bf16[512,1024]{1,0:T(8,128)(2,1)S(1)} %get-tuple-element.35.z.z_low, bf16[512,256]{1,0:T(8,128)(2,1)S(1)} %collective-permute-done.4.left, bf16[512,256]{1,0:T(8,128)(2,1)S(1)} %collective-permute-done.5.lower), custom_call_target="tpu_custom_call" | custom-call | flops 536870912 | bytes 3145728 | tf_op jit(solution)/shard_map/last/pallas_call | solution.py:293
  39.8 0.2 collective-permute-done.10.left
  40.0 0.9 %collective-permute-done.11.lower = bf16[512,256]{1,0:T(8,128)(2,1)S(1)} collective-permute-done((bf16[512,256]{1,0:T(8,128)(2,1)S(1)}, bf16[512,256]{1,0:T(8,128)(2,1)S(1)}, u32[]{:S(2)}, u32[]{:S(2)}) %collective-permute-start.11) | collective-permute-done | bytes 262176 | tf_op jit(solution)/shard_map/ppermute | solution.py:21
  40.8 0.2 edges.1
  41.0 1.7 %collective-permute-start.12 = (bf16[16,512]{1,0:T(8,128)(2,1)S(1)}, bf16[16,512]{1,0:T(8,128)(2,1)S(1)}, u32[]{:S(2)}, u32[]{:S(2)}) collective-permute-start(bf16[16,512]{1,0:T(8,128)(2,1)S(1)} %get-tuple-element.54), channel_id=1, source_target_pairs={{0,4},{1,5},{2,6},{3,7},{4,0},{5,1},{6,2},{7,3},{8,12},{9,13},{10,... | collective-permute-start | bytes 49160 | tf_op jit(solution)/shard_map/ppermute | solution.py:44
  42.7 0.0 collective-permute-start.13
  42.7 0.5 %collective-permute-start.14 = (bf16[16,512]{1,0:T(8,128)(2,1)S(1)}, bf16[16,512]{1,0:T(8,128)(2,1)S(1)}, u32[]{:S(2)}, u32[]{:S(2)}) collective-permute-start(bf16[16,512]{1,0:T(8,128)(2,1)S(1)} %get-tuple-element.56), channel_id=1, source_target_pairs={{0,1},{1,0},{2,3},{3,2},{4,5},{5,4},{6,7},{7,6},{8,9},{9,8},{10,11... | collective-permute-start | bytes 49160 | tf_op jit(solution)/shard_map/ppermute | solution.py:44
  43.2 0.9 %collective-permute-start.15 = (bf16[16,512]{1,0:T(8,128)(2,1)S(1)}, bf16[16,512]{1,0:T(8,128)(2,1)S(1)}, u32[]{:S(2)}, u32[]{:S(2)}) collective-permute-start(bf16[16,512]{1,0:T(8,128)(2,1)S(1)} %get-tuple-element.57), channel_id=1, source_target_pairs={{0,3},{1,2},{2,1},{3,0},{4,7},{5,6},{6,5},{7,4},{8,11},{9,10},{10,... | collective-permute-start | bytes 49160 | tf_op jit(solution)/shard_map/ppermute | solution.py:44
  44.2 1.4 %plain.1 = (bf16[512,512]{1,0:T(8,128)(2,1)}, f32[16,16,512]{2,1,0:T(8,128)S(1)}, bf16[512,256]{1,0:T(8,128)(2,1)S(1)}) custom-call(bf16[512,1024]{1,0:T(8,128)(2,1)S(1)} %get-tuple-element.32.z.z_top, bf16[512,1024]{1,0:T(8,128)(2,1)S(1)} %get-tuple-element.35.z.z_low, bf16[256,1024]{1,0:T(8,128)(2,1)S(1)} %bitcast.7, ...), custom_call_target="tpu_custom_call", output_to_operand_aliasing={{0}: (7, {})} | custom-call | flops 536870912 | bytes 3145728 | tf_op jit(solution)/shard_map/plain/pallas_call | solution.py:351
  45.5 0.0 collective-permute-done.12.x_pair
  45.5 0.0 collective-permute-done.13.x_cross
  45.6 0.0 collective-permute-done.14.y_pair
  45.6 0.8 %collective-permute-done.15.y_cross = bf16[16,512]{1,0:T(8,128)(2,1)S(1)} collective-permute-done((bf16[16,512]{1,0:T(8,128)(2,1)S(1)}, bf16[16,512]{1,0:T(8,128)(2,1)S(1)}, u32[]{:S(2)}, u32[]{:S(2)}) %collective-permute-start.15) | collective-permute-done | bytes 16416 | tf_op jit(solution)/shard_map/ppermute | solution.py:44
  46.4 0.9 %finish.1 = (bf16[512,512]{1,0:T(8,128)(2,1)}, f32[16,16,512]{2,1,0:T(8,128)}) custom-call(f32[16,16,512]{2,1,0:T(8,128)S(1)} %get-tuple-element.50.inner, bf16[512,256]{1,0:T(8,128)(2,1)S(1)} %get-tuple-element.51.upper, bf16[16,512]{1,0:T(8,128)(2,1)S(1)} %collective-permute-done.12.x_pair, ...), custom_call_target="tpu_custom_call", output_to_operand_aliasing={{0}: (6, {})} | custom-call | flops 524288 | bytes 1048576 | tf_op jit(solution)/shard_map/finish/pallas_call | solution.py:413
Async XLA Ops:
  2.7 12.4 %collective-permute-start = (bf16[512,256]{1,0:T(8,128)(2,1)S(1)}, bf16[512,256]{1,0:T(8,128)(2,1)S(1)}, u32[]{:S(2)}, u32[]{:S(2)}) collective-permute-start(bf16[512,256]{1,0:T(8,128)(2,1)S(1)} %get-tuple-element.36), channel_id=1, source_target_pairs={{0,4},{4,8},{8,12},{12,16},{16,20},{20,24},{24,28},{28,0},{1,5},{5... | collective-permute-start | bytes 786440 | tf_op jit(solution)/shard_map/ppermute | solution.py:21
  7.6 7.4 %collective-permute-start.1 = (bf16[512,256]{1,0:T(8,128)(2,1)S(1)}, bf16[512,256]{1,0:T(8,128)(2,1)S(1)}, u32[]{:S(2)}, u32[]{:S(2)}) collective-permute-start(bf16[512,256]{1,0:T(8,128)(2,1)S(1)} %get-tuple-element.37), channel_id=1, source_target_pairs={{0,1},{1,2},{2,3},{3,0},{4,5},{5,6},{6,7},{7,4},{8,9},{9,10},{10,1... | collective-permute-start | bytes 786440 | tf_op jit(solution)/shard_map/ppermute | solution.py:21
  9.2 11.3 %collective-permute-start.6 = (bf16[512,256]{1,0:T(8,128)(2,1)S(1)}, bf16[512,256]{1,0:T(8,128)(2,1)S(1)}, u32[]{:S(2)}, u32[]{:S(2)}) collective-permute-start(bf16[512,256]{1,0:T(8,128)(2,1)S(1)} %get-tuple-element.39), channel_id=1, source_target_pairs={{0,4},{4,8},{8,12},{12,16},{16,20},{20,24},{24,28},{28,0},{1,5},{5... | collective-permute-start | bytes 786440 | tf_op jit(solution)/shard_map/ppermute | solution.py:21
  11.2 9.2 %collective-permute-start.7 = (bf16[512,256]{1,0:T(8,128)(2,1)S(1)}, bf16[512,256]{1,0:T(8,128)(2,1)S(1)}, u32[]{:S(2)}, u32[]{:S(2)}) collective-permute-start(bf16[512,256]{1,0:T(8,128)(2,1)S(1)} %part.13), channel_id=1, source_target_pairs={{0,1},{1,2},{2,3},{3,0},{4,5},{5,6},{6,7},{7,4},{8,9},{9,10},{10,1... | collective-permute-start | bytes 786440 | tf_op jit(solution)/shard_map/ppermute | solution.py:21
  15.5 11.2 %collective-permute-start.2 = (bf16[512,256]{1,0:T(8,128)(2,1)S(1)}, bf16[512,256]{1,0:T(8,128)(2,1)S(1)}, u32[]{:S(2)}, u32[]{:S(2)}) collective-permute-start(bf16[512,256]{1,0:T(8,128)(2,1)S(1)} %part.9), channel_id=1, source_target_pairs={{0,4},{4,8},{8,12},{12,16},{16,20},{20,24},{24,28},{28,0},{1,5},{5... | collective-permute-start | bytes 786440 | tf_op jit(solution)/shard_map/ppermute | solution.py:21
  16.0 10.7 %collective-permute-start.3 = (bf16[512,256]{1,0:T(8,128)(2,1)S(1)}, bf16[512,256]{1,0:T(8,128)(2,1)S(1)}, u32[]{:S(2)}, u32[]{:S(2)}) collective-permute-start(bf16[512,256]{1,0:T(8,128)(2,1)S(1)} %part.10), channel_id=1, source_target_pairs={{0,1},{1,2},{2,3},{3,0},{4,5},{5,6},{6,7},{7,4},{8,9},{9,10},{10,1... | collective-permute-start | bytes 786440 | tf_op jit(solution)/shard_map/ppermute | solution.py:21
  20.9 11.9 %collective-permute-start.8 = (bf16[512,256]{1,0:T(8,128)(2,1)S(1)}, bf16[512,256]{1,0:T(8,128)(2,1)S(1)}, u32[]{:S(2)}, u32[]{:S(2)}) collective-permute-start(bf16[512,256]{1,0:T(8,128)(2,1)S(1)} %part.14), channel_id=1, source_target_pairs={{0,4},{4,8},{8,12},{12,16},{16,20},{20,24},{24,28},{28,0},{1,5},{5... | collective-permute-start | bytes 786440 | tf_op jit(solution)/shard_map/ppermute | solution.py:21
  21.4 11.3 %collective-permute-start.9 = (bf16[512,256]{1,0:T(8,128)(2,1)S(1)}, bf16[512,256]{1,0:T(8,128)(2,1)S(1)}, u32[]{:S(2)}, u32[]{:S(2)}) collective-permute-start(bf16[512,256]{1,0:T(8,128)(2,1)S(1)} %part.15), channel_id=1, source_target_pairs={{0,1},{1,2},{2,3},{3,0},{4,5},{5,6},{6,7},{7,4},{8,9},{9,10},{10,1... | collective-permute-start | bytes 786440 | tf_op jit(solution)/shard_map/ppermute | solution.py:21
  27.2 10.8 %collective-permute-start.4 = (bf16[512,256]{1,0:T(8,128)(2,1)S(1)}, bf16[512,256]{1,0:T(8,128)(2,1)S(1)}, u32[]{:S(2)}, u32[]{:S(2)}) collective-permute-start(bf16[512,256]{1,0:T(8,128)(2,1)S(1)} %part.11), channel_id=1, source_target_pairs={{0,4},{4,8},{8,12},{12,16},{16,20},{20,24},{24,28},{28,0},{1,5},{5... | collective-permute-start | bytes 786440 | tf_op jit(solution)/shard_map/ppermute | solution.py:21
  27.7 7.3 %copy-start.1 = (s32[16,16]{1,0:T(8,128)S(1)}, s32[16,16]{1,0:T(8,128)}, u32[]{:S(2)}) copy-start(s32[16,16]{1,0:T(8,128)} %kinds.1) | copy-start | bytes 3076
  27.7 7.3 %copy-start.2 = (f32[16]{0:T(128)S(1)}, f32[16]{0:T(128)}, u32[]{:S(2)}) copy-start(f32[16]{0:T(128)} %table.1) | copy-start | bytes 196
  27.7 10.3 %copy-start = (bf16[1,1,256,1024]{3,2,1,0:T(8,128)(2,1)S(1)}, bf16[1,1,256,1024]{3,2,1,0:T(8,128)(2,1)}, u32[]{:S(2)}) copy-start(bf16[1,1,256,1024]{3,2,1,0:T(8,128)(2,1)} %param.7) | copy-start | bytes 1572868
  27.7 10.2 %collective-permute-start.5 = (bf16[512,256]{1,0:T(8,128)(2,1)S(1)}, bf16[512,256]{1,0:T(8,128)(2,1)S(1)}, u32[]{:S(2)}, u32[]{:S(2)}) collective-permute-start(bf16[512,256]{1,0:T(8,128)(2,1)S(1)} %part.12), channel_id=1, source_target_pairs={{0,1},{1,2},{2,3},{3,0},{4,5},{5,6},{6,7},{7,4},{8,9},{9,10},{10,1... | collective-permute-start | bytes 786440 | tf_op jit(solution)/shard_map/ppermute | solution.py:21
  33.2 6.7 %collective-permute-start.10 = (bf16[512,256]{1,0:T(8,128)(2,1)S(1)}, bf16[512,256]{1,0:T(8,128)(2,1)S(1)}, u32[]{:S(2)}, u32[]{:S(2)}) collective-permute-start(bf16[512,256]{1,0:T(8,128)(2,1)S(1)} %part.16), channel_id=1, source_target_pairs={{0,4},{4,8},{8,12},{12,16},{16,20},{20,24},{24,28},{1,5},{5,9},{9,... | collective-permute-start | bytes 786440 | tf_op jit(solution)/shard_map/ppermute | solution.py:26
  35.0 5.8 %collective-permute-start.11 = (bf16[512,256]{1,0:T(8,128)(2,1)S(1)}, bf16[512,256]{1,0:T(8,128)(2,1)S(1)}, u32[]{:S(2)}, u32[]{:S(2)}) collective-permute-start(bf16[512,256]{1,0:T(8,128)(2,1)S(1)} %part.17), channel_id=1, source_target_pairs={{0,1},{1,2},{2,3},{3,0},{4,5},{5,6},{6,7},{7,4},{8,9},{9,10},{10,1... | collective-permute-start | bytes 786440 | tf_op jit(solution)/shard_map/ppermute | solution.py:21
  41.0 4.5 %collective-permute-start.12 = (bf16[16,512]{1,0:T(8,128)(2,1)S(1)}, bf16[16,512]{1,0:T(8,128)(2,1)S(1)}, u32[]{:S(2)}, u32[]{:S(2)}) collective-permute-start(bf16[16,512]{1,0:T(8,128)(2,1)S(1)} %get-tuple-element.54), channel_id=1, source_target_pairs={{0,4},{1,5},{2,6},{3,7},{4,0},{5,1},{6,2},{7,3},{8,12},{9,13},{10,... | collective-permute-start | bytes 49160 | tf_op jit(solution)/shard_map/ppermute | solution.py:44
  42.7 2.8 %collective-permute-start.13 = (bf16[16,512]{1,0:T(8,128)(2,1)S(1)}, bf16[16,512]{1,0:T(8,128)(2,1)S(1)}, u32[]{:S(2)}, u32[]{:S(2)}) collective-permute-start(bf16[16,512]{1,0:T(8,128)(2,1)S(1)} %get-tuple-element.55), channel_id=1, source_target_pairs={{0,1},{1,0},{2,3},{3,2},{4,8},{5,9},{6,10},{7,11},{8,4},{9,5},{10,... | collective-permute-start | bytes 49160 | tf_op jit(solution)/shard_map/ppermute | solution.py:44
  42.7 2.8 %collective-permute-start.14 = (bf16[16,512]{1,0:T(8,128)(2,1)S(1)}, bf16[16,512]{1,0:T(8,128)(2,1)S(1)}, u32[]{:S(2)}, u32[]{:S(2)}) collective-permute-start(bf16[16,512]{1,0:T(8,128)(2,1)S(1)} %get-tuple-element.56), channel_id=1, source_target_pairs={{0,1},{1,0},{2,3},{3,2},{4,5},{5,4},{6,7},{7,6},{8,9},{9,8},{10,11... | collective-permute-start | bytes 49160 | tf_op jit(solution)/shard_map/ppermute | solution.py:44
  43.2 3.2 %collective-permute-start.15 = (bf16[16,512]{1,0:T(8,128)(2,1)S(1)}, bf16[16,512]{1,0:T(8,128)(2,1)S(1)}, u32[]{:S(2)}, u32[]{:S(2)}) collective-permute-start(bf16[16,512]{1,0:T(8,128)(2,1)S(1)} %get-tuple-element.57), channel_id=1, source_target_pairs={{0,3},{1,2},{2,1},{3,0},{4,7},{5,6},{6,5},{7,4},{8,11},{9,10},{10,... | collective-permute-start | bytes 49160 | tf_op jit(solution)/shard_map/ppermute | solution.py:44
where the time goes:
time: 47.5 us; the launch traced here: 47.3 us
  waiting for transfers between devices  20.7 us (44%)
  Pallas kernels  14.3 us (30%)
  starting transfers between devices  11.4 us (24%)
  between operations  0.89 us (2%)
    ppermute x11, waiting for transfers between devices, around(): lax.ppermute(block, axis, [(i, (i + 1) % count) for i in range(count)])  19.7 us
    ppermute x11, starting transfers between devices, around(): lax.ppermute(block, axis, [(i, (i + 1) % count) for i in range(count)])  6.94 us
    pallas_call x9, Pallas kernels, part(): pl.pallas_call(functools.partial(part_kernel, axis), out_shape=jax.ShapeD...  3.92 us
    ppermute x4, starting transfers between devices, swapped(): return lax.ppermute(block, names, pairs)  3.12 us
    pallas_call x1, Pallas kernels, first_right(): pl.pallas_call(functools.partial(first_right_kernel, base, width), out_sh...  2.05 us
    pallas_call x1, Pallas kernels, first_upper(): pl.pallas_call(first_upper_kernel, out_shape=(vmem(trace, width), vmem(tr...  1.9 us
    pallas_call x1, Pallas kernels, part_loading(): pl.pallas_call(functools.partial(part_loading_kernel, axis, base), out_sh...  1.49 us
    pallas_call x1, Pallas kernels, last(): pl.pallas_call(last_kernel, out_shape=(out, out), in_specs=[VMEM] * 4, ou...  1.45 us
  transfers between devices with their start and end apart: 16, of which 8 were waited for; matrix products, arithmetic and copies ran while one was open for 0% of the time, Pallas kernels for 24%

commit v1 on v0

--- a/solution.py
+++ b/solution.py
@@ -68,20 +68,23 @@
 
 def first_right_kernel(base, width, z_hbm, left_hbm, lower_hbm, out, z_top, left, lower, sem):
     rows = z_top.shape[0]
-    split = rows * 6 // 8
-    blocks = (pl.ds(0, split), pl.ds(split, rows - split))
+    block = rows // 2
     loads = [
         pltpu.make_async_copy(left_hbm.at[:, pl.ds(base, width)], left, sem.at[0]),
         pltpu.make_async_copy(lower_hbm.at[:, pl.ds(base, width)], lower, sem.at[1]),
     ]
-    parts = [pltpu.make_async_copy(z_hbm.at[here], z_top.at[here], sem.at[2 + r]) for r, here in enumerate(blocks)]
+    parts = [
+        pltpu.make_async_copy(z_hbm.at[pl.ds(r * block, block)], z_top.at[pl.ds(r * block, block)], sem.at[2 + r])
+        for r in range(2)
+    ]
     for copy in loads + parts:
         copy.start()
     for copy in loads:
         copy.wait()
     at_end = is_last("gx")
-    for copy, here in zip(parts, blocks):
-        copy.wait()
+    for r in range(2):
+        parts[r].wait()
+        here = pl.ds(r * block, block)
         out[here] = jnp.where(at_end, 0.0, product(z_top.at[here], [left], lower)).astype(BF16)
 
 
@@ -95,7 +98,7 @@
         out_specs=(VMEM,) * 4,
         scratch_shapes=[pltpu.SemaphoreType.DMA((4,))],
         cost_estimate=cost(4 * trace * trace * width, 4 * trace * trace + 6 * trace * width),
-        compiler_params=PARAMS,
+        compiler_params=PACKED,
         name="first_right",
     )(z, left, lower)
 
@@ -147,7 +150,7 @@
         in_specs=[VMEM] * 3,
         out_specs=VMEM,
         cost_estimate=cost(4 * trace * trace * width, 4 * trace * trace + 6 * trace * width),
-        compiler_params=PARAMS,
+        compiler_params=PACKED,
         name="part",
     )(z, left, lower)
 
@@ -175,7 +178,7 @@
         out_specs=(VMEM,) * 3,
         scratch_shapes=[pltpu.SemaphoreType.DMA((2,))],
         cost_estimate=cost(4 * trace * trace * width, 4 * trace * trace + 6 * trace * width),
-        compiler_params=PARAMS,
+        compiler_params=PACKED,
         name="part_loading",
     )(z, left, lower)
 
@@ -266,7 +269,7 @@
         in_specs=[VMEM] * 4,
         out_specs=(VMEM,) * 4,
         cost_estimate=cost(2 * weights.size * width, 2 * weights.size + 4 * weights.shape[1] * width),
-        compiler_params=PARAMS,
+        compiler_params=PACKED,
         name="edges",
     )(weights, left, lower, done)
 
@@ -301,7 +304,7 @@
             pltpu.SemaphoreType.DMA((4,)),
         ],
         cost_estimate=cost(8 * trace * trace * width, 8 * trace * trace + 8 * trace * width),
-        compiler_params=PARAMS,
+        compiler_params=PACKED,
         name="last",
     )(z_top, z_low, left, lower)
 

time: 47.5 us -> 47.6 us (level)
  no operation moved by 1% of the time
where the time goes in v1:
time: 47.6 us; the launch traced here: 47.3 us
  waiting for transfers between devices  20.7 us (43%)
  Pallas kernels  14.3 us (30%)
  starting transfers between devices  11.4 us (24%)
  between operations  0.89 us (2%)
    ppermute x11, waiting for transfers between devices, around(): lax.ppermute(block, axis, [(i, (i + 1) % count) for i in range(count)])  19.7 us
    ppermute x11, starting transfers between devices, around(): lax.ppermute(block, axis, [(i, (i + 1) % count) for i in range(count)])  6.93 us
    pallas_call x9, Pallas kernels, part(): pl.pallas_call(functools.partial(part_kernel, axis), out_shape=jax.ShapeD...  3.92 us
    ppermute x4, starting transfers between devices, swapped(): return lax.ppermute(block, names, pairs)  3.13 us
    pallas_call x1, Pallas kernels, first_right(): pl.pallas_call(functools.partial(first_right_kernel, base, width), out_sh...  2.08 us
    pallas_call x1, Pallas kernels, first_upper(): pl.pallas_call(first_upper_kernel, out_shape=(vmem(trace, width), vmem(tr...  1.9 us
    pallas_call x1, Pallas kernels, part_loading(): pl.pallas_call(functools.partial(part_loading_kernel, axis, base), out_sh...  1.49 us
    pallas_call x1, Pallas kernels, last(): pl.pallas_call(last_kernel, out_shape=(out, out), in_specs=[VMEM] * 4, ou...  1.45 us
  transfers between devices with their start and end apart: 16, of which 8 were waited for; matrix products, arithmetic and copies ran while one was open for 0% of the time, Pallas kernels for 24%

profile of v1, /device:TPU:0, one launch (start us, length us, event | category | flops | bytes accessed | tf_op | source)
XLA Modules:
  0.0 47.3 jit_solution(3628220227022755036)
XLA Ops:
  0.6 2.1 %first_right.1 = (bf16[512,256]{1,0:T(8,128)(2,1)S(1)}, bf16[512,1024]{1,0:T(8,128)(2,1)S(1)}, bf16[512,256]{1,0:T(8,128)(2,1)S(1)}, bf16[512,256]{1,0:T(8,128)(2,1)S(1)}) custom-call(bf16[1024,1024]{1,0:T(8,128)(2,1)} %bitcast.8, bf16[512,512]{1,0:T(8,128)(2,1)} %bitcast.10, bf16[512,512]{1,0:T(8,128)(2,1)} %bitcast.12), custom_call_target="tpu_custom_call" | custom-call | flops 268435456 | bytes 1835008 | tf_op jit(solution)/shard_map/first_right/pallas_call | solution.py:94
  2.7 3.0 %collective-permute-start = (bf16[512,256]{1,0:T(8,128)(2,1)S(1)}, bf16[512,256]{1,0:T(8,128)(2,1)S(1)}, u32[]{:S(2)}, u32[]{:S(2)}) collective-permute-start(bf16[512,256]{1,0:T(8,128)(2,1)S(1)} %get-tuple-element.36), channel_id=1, source_target_pairs={{0,4},{4,8},{8,12},{12,16},{16,20},{20,24},{24,28},{28,0},{1,5},{5... | collective-permute-start | bytes 786440 | tf_op jit(solution)/shard_map/ppermute | solution.py:21
  5.7 1.9 %first_upper.1 = (bf16[512,256]{1,0:T(8,128)(2,1)S(1)}, bf16[512,1024]{1,0:T(8,128)(2,1)S(1)}) custom-call(bf16[1024,1024]{1,0:T(8,128)(2,1)} %bitcast.9, bf16[512,256]{1,0:T(8,128)(2,1)S(1)} %get-tuple-element.33.left, bf16[512,256]{1,0:T(8,128)(2,1)S(1)} %get-tuple-element.34.lower), custom_call_target="tpu_custom_call" | custom-call | flops 268435456 | bytes 1835008 | tf_op jit(solution)/shard_map/first_upper/pallas_call | solution.py:125
  7.6 0.1 collective-permute-start.1
  7.7 1.5 %part_loading.1 = (bf16[512,256]{1,0:T(8,128)(2,1)S(1)}, bf16[512,256]{1,0:T(8,128)(2,1)S(1)}, bf16[512,256]{1,0:T(8,128)(2,1)S(1)}) custom-call(bf16[512,1024]{1,0:T(8,128)(2,1)S(1)} %get-tuple-element.32.z.z_top, bf16[512,512]{1,0:T(8,128)(2,1)} %bitcast.11, bf16[512,512]{1,0:T(8,128)(2,1)} %bitcast.13), custom_call_target="tpu_custom_call" | custom-call | flops 268435456 | bytes 1835008 | tf_op jit(solution)/shard_map/part_loading/pallas_call | solution.py:174
  9.2 1.6 %collective-permute-start.6 = (bf16[512,256]{1,0:T(8,128)(2,1)S(1)}, bf16[512,256]{1,0:T(8,128)(2,1)S(1)}, u32[]{:S(2)}, u32[]{:S(2)}) collective-permute-start(bf16[512,256]{1,0:T(8,128)(2,1)S(1)} %get-tuple-element.39), channel_id=1, source_target_pairs={{0,4},{4,8},{8,12},{12,16},{16,20},{20,24},{24,28},{28,0},{1,5},{5... | collective-permute-start | bytes 786440 | tf_op jit(solution)/shard_map/ppermute | solution.py:21
  10.8 0.4 part.13
  11.3 1.4 %collective-permute-start.7 = (bf16[512,256]{1,0:T(8,128)(2,1)S(1)}, bf16[512,256]{1,0:T(8,128)(2,1)S(1)}, u32[]{:S(2)}, u32[]{:S(2)}) collective-permute-start(bf16[512,256]{1,0:T(8,128)(2,1)S(1)} %part.13), channel_id=1, source_target_pairs={{0,1},{1,2},{2,3},{3,0},{4,5},{5,6},{6,7},{7,4},{8,9},{9,10},{10,1... | collective-permute-start | bytes 786440 | tf_op jit(solution)/shard_map/ppermute | solution.py:21
  12.6 2.4 %collective-permute-done.left = bf16[512,256]{1,0:T(8,128)(2,1)S(1)} collective-permute-done((bf16[512,256]{1,0:T(8,128)(2,1)S(1)}, bf16[512,256]{1,0:T(8,128)(2,1)S(1)}, u32[]{:S(2)}, u32[]{:S(2)}) %collective-permute-start) | collective-permute-done | bytes 262176 | tf_op jit(solution)/shard_map/ppermute | solution.py:21
  15.1 0.0 collective-permute-done.1.lower
  15.1 0.4 part.9
  15.5 0.1 collective-permute-start.2
  15.6 0.4 part.10
  16.0 0.1 collective-permute-start.3
  16.1 4.4 %collective-permute-done.6.left = bf16[512,256]{1,0:T(8,128)(2,1)S(1)} collective-permute-done((bf16[512,256]{1,0:T(8,128)(2,1)S(1)}, bf16[512,256]{1,0:T(8,128)(2,1)S(1)}, u32[]{:S(2)}, u32[]{:S(2)}) %collective-permute-start.6) | collective-permute-done | bytes 262176 | tf_op jit(solution)/shard_map/ppermute | solution.py:21
  20.5 0.0 collective-permute-done.7.lower
  20.5 0.4 part.14
  20.9 0.1 collective-permute-start.8
  21.0 0.4 part.15
  21.4 0.5 %collective-permute-start.9 = (bf16[512,256]{1,0:T(8,128)(2,1)S(1)}, bf16[512,256]{1,0:T(8,128)(2,1)S(1)}, u32[]{:S(2)}, u32[]{:S(2)}) collective-permute-start(bf16[512,256]{1,0:T(8,128)(2,1)S(1)} %part.15), channel_id=1, source_target_pairs={{0,1},{1,2},{2,3},{3,0},{4,5},{5,6},{6,7},{7,4},{8,9},{9,10},{10,1... | collective-permute-start | bytes 786440 | tf_op jit(solution)/shard_map/ppermute | solution.py:21
  22.0 4.8 %collective-permute-done.2.left = bf16[512,256]{1,0:T(8,128)(2,1)S(1)} collective-permute-done((bf16[512,256]{1,0:T(8,128)(2,1)S(1)}, bf16[512,256]{1,0:T(8,128)(2,1)S(1)}, u32[]{:S(2)}, u32[]{:S(2)}) %collective-permute-start.2) | collective-permute-done | bytes 262176 | tf_op jit(solution)/shard_map/ppermute | solution.py:21
  26.8 0.0 collective-permute-done.3.lower
  26.8 0.4 part.11
  27.2 0.1 collective-permute-start.4
  27.3 0.4 part.12
  27.7 0.0 copy-start.1
  27.7 0.0 copy-start.2
  27.7 0.0 copy-start
  27.8 0.1 collective-permute-start.5
  27.8 5.0 %collective-permute-done.8.left = bf16[512,256]{1,0:T(8,128)(2,1)S(1)} collective-permute-done((bf16[512,256]{1,0:T(8,128)(2,1)S(1)}, bf16[512,256]{1,0:T(8,128)(2,1)S(1)}, u32[]{:S(2)}, u32[]{:S(2)}) %collective-permute-start.8) | collective-permute-done | bytes 262176 | tf_op jit(solution)/shard_map/ppermute | solution.py:21
  32.8 0.0 collective-permute-done.9.lower
  32.8 0.4 part.16
  33.2 1.3 %collective-permute-start.10 = (bf16[512,256]{1,0:T(8,128)(2,1)S(1)}, bf16[512,256]{1,0:T(8,128)(2,1)S(1)}, u32[]{:S(2)}, u32[]{:S(2)}) collective-permute-start(bf16[512,256]{1,0:T(8,128)(2,1)S(1)} %part.16), channel_id=1, source_target_pairs={{0,4},{4,8},{8,12},{12,16},{16,20},{20,24},{24,28},{1,5},{5,9},{9,... | collective-permute-start | bytes 786440 | tf_op jit(solution)/shard_map/ppermute | solution.py:26
  34.6 0.4 part.17
  35.0 0.1 collective-permute-start.11
  35.1 0.0 copy-done.1
  35.1 0.0 copy-done.2
  35.1 0.7 %wavenum.1 = f32[256,128]{1,0:T(8,128)S(1)} custom-call(f32[16]{0:T(128)S(1)} %copy-done.2, s32[16,16]{1,0:T(8,128)S(1)} %copy-done.1), custom_call_target="tpu_custom_call" | custom-call | tf_op jit(solution)/shard_map/wavenum/pallas_call | solution.py:200
  35.7 2.3 %collective-permute-done.4.left = bf16[512,256]{1,0:T(8,128)(2,1)S(1)} collective-permute-done((bf16[512,256]{1,0:T(8,128)(2,1)S(1)}, bf16[512,256]{1,0:T(8,128)(2,1)S(1)}, u32[]{:S(2)}, u32[]{:S(2)}) %collective-permute-start.4) | collective-permute-done | bytes 262176 | tf_op jit(solution)/shard_map/ppermute | solution.py:21
  38.0 0.0 collective-permute-done.5.lower
  38.0 0.0 copy-done
  38.0 0.4 volume.1
  38.4 1.4 %last.1 = (bf16[512,512]{1,0:T(8,128)(2,1)}, bf16[512,512]{1,0:T(8,128)(2,1)}) custom-call(bf16[512,1024]{1,0:T(8,128)(2,1)S(1)} %get-tuple-element.32.z.z_top, bf16[512,1024]{1,0:T(8,128)(2,1)S(1)} %get-tuple-element.35.z.z_low, bf16[512,256]{1,0:T(8,128)(2,1)S(1)} %collective-permute-done.4.left, bf16[512,256]{1,0:T(8,128)(2,1)S(1)} %collective-permute-done.5.lower), custom_call_target="tpu_custom_call" | custom-call | flops 536870912 | bytes 3145728 | tf_op jit(solution)/shard_map/last/pallas_call | solution.py:296
  39.8 0.2 collective-permute-done.10.left
  40.0 0.9 %collective-permute-done.11.lower = bf16[512,256]{1,0:T(8,128)(2,1)S(1)} collective-permute-done((bf16[512,256]{1,0:T(8,128)(2,1)S(1)}, bf16[512,256]{1,0:T(8,128)(2,1)S(1)}, u32[]{:S(2)}, u32[]{:S(2)}) %collective-permute-start.11) | collective-permute-done | bytes 262176 | tf_op jit(solution)/shard_map/ppermute | solution.py:21
  40.8 0.2 edges.1
  41.1 1.7 %collective-permute-start.12 = (bf16[16,512]{1,0:T(8,128)(2,1)S(1)}, bf16[16,512]{1,0:T(8,128)(2,1)S(1)}, u32[]{:S(2)}, u32[]{:S(2)}) collective-permute-start(bf16[16,512]{1,0:T(8,128)(2,1)S(1)} %get-tuple-element.54), channel_id=1, source_target_pairs={{0,4},{1,5},{2,6},{3,7},{4,0},{5,1},{6,2},{7,3},{8,12},{9,13},{10,... | collective-permute-start | bytes 49160 | tf_op jit(solution)/shard_map/ppermute | solution.py:44
  42.7 0.0 collective-permute-start.13
  42.8 0.5 %collective-permute-start.14 = (bf16[16,512]{1,0:T(8,128)(2,1)S(1)}, bf16[16,512]{1,0:T(8,128)(2,1)S(1)}, u32[]{:S(2)}, u32[]{:S(2)}) collective-permute-start(bf16[16,512]{1,0:T(8,128)(2,1)S(1)} %get-tuple-element.56), channel_id=1, source_target_pairs={{0,1},{1,0},{2,3},{3,2},{4,5},{5,4},{6,7},{7,6},{8,9},{9,8},{10,11... | collective-permute-start | bytes 49160 | tf_op jit(solution)/shard_map/ppermute | solution.py:44
  43.3 0.9 %collective-permute-start.15 = (bf16[16,512]{1,0:T(8,128)(2,1)S(1)}, bf16[16,512]{1,0:T(8,128)(2,1)S(1)}, u32[]{:S(2)}, u32[]{:S(2)}) collective-permute-start(bf16[16,512]{1,0:T(8,128)(2,1)S(1)} %get-tuple-element.57), channel_id=1, source_target_pairs={{0,3},{1,2},{2,1},{3,0},{4,7},{5,6},{6,5},{7,4},{8,11},{9,10},{10,... | collective-permute-start | bytes 49160 | tf_op jit(solution)/shard_map/ppermute | solution.py:44
  44.2 1.4 %plain.1 = (bf16[512,512]{1,0:T(8,128)(2,1)}, f32[16,16,512]{2,1,0:T(8,128)S(1)}, bf16[512,256]{1,0:T(8,128)(2,1)S(1)}) custom-call(bf16[512,1024]{1,0:T(8,128)(2,1)S(1)} %get-tuple-element.32.z.z_top, bf16[512,1024]{1,0:T(8,128)(2,1)S(1)} %get-tuple-element.35.z.z_low, bf16[256,1024]{1,0:T(8,128)(2,1)S(1)} %bitcast.7, ...), custom_call_target="tpu_custom_call", output_to_operand_aliasing={{0}: (7, {})} | custom-call | flops 536870912 | bytes 3145728 | tf_op jit(solution)/shard_map/plain/pallas_call | solution.py:354
  45.6 0.0 collective-permute-done.12.x_pair
  45.6 0.0 collective-permute-done.13.x_cross
  45.6 0.0 collective-permute-done.14.y_pair
  45.6 0.8 %collective-permute-done.15.y_cross = bf16[16,512]{1,0:T(8,128)(2,1)S(1)} collective-permute-done((bf16[16,512]{1,0:T(8,128)(2,1)S(1)}, bf16[16,512]{1,0:T(8,128)(2,1)S(1)}, u32[]{:S(2)}, u32[]{:S(2)}) %collective-permute-start.15) | collective-permute-done | bytes 16416 | tf_op jit(solution)/shard_map/ppermute | solution.py:44
  46.4 0.9 %finish.1 = (bf16[512,512]{1,0:T(8,128)(2,1)}, f32[16,16,512]{2,1,0:T(8,128)}) custom-call(f32[16,16,512]{2,1,0:T(8,128)S(1)} %get-tuple-element.50.inner, bf16[512,256]{1,0:T(8,128)(2,1)S(1)} %get-tuple-element.51.upper, bf16[16,512]{1,0:T(8,128)(2,1)S(1)} %collective-permute-done.12.x_pair, ...), custom_call_target="tpu_custom_call", output_to_operand_aliasing={{0}: (6, {})} | custom-call | flops 524288 | bytes 1048576 | tf_op jit(solution)/shard_map/finish/pallas_call | solution.py:416
Async XLA Ops:
  2.7 12.4 %collective-permute-start = (bf16[512,256]{1,0:T(8,128)(2,1)S(1)}, bf16[512,256]{1,0:T(8,128)(2,1)S(1)}, u32[]{:S(2)}, u32[]{:S(2)}) collective-permute-start(bf16[512,256]{1,0:T(8,128)(2,1)S(1)} %get-tuple-element.36), channel_id=1, source_target_pairs={{0,4},{4,8},{8,12},{12,16},{16,20},{20,24},{24,28},{28,0},{1,5},{5... | collective-permute-start | bytes 786440 | tf_op jit(solution)/shard_map/ppermute | solution.py:21
  7.6 7.4 %collective-permute-start.1 = (bf16[512,256]{1,0:T(8,128)(2,1)S(1)}, bf16[512,256]{1,0:T(8,128)(2,1)S(1)}, u32[]{:S(2)}, u32[]{:S(2)}) collective-permute-start(bf16[512,256]{1,0:T(8,128)(2,1)S(1)} %get-tuple-element.37), channel_id=1, source_target_pairs={{0,1},{1,2},{2,3},{3,0},{4,5},{5,6},{6,7},{7,4},{8,9},{9,10},{10,1... | collective-permute-start | bytes 786440 | tf_op jit(solution)/shard_map/ppermute | solution.py:21
  9.2 11.3 %collective-permute-start.6 = (bf16[512,256]{1,0:T(8,128)(2,1)S(1)}, bf16[512,256]{1,0:T(8,128)(2,1)S(1)}, u32[]{:S(2)}, u32[]{:S(2)}) collective-permute-start(bf16[512,256]{1,0:T(8,128)(2,1)S(1)} %get-tuple-element.39), channel_id=1, source_target_pairs={{0,4},{4,8},{8,12},{12,16},{16,20},{20,24},{24,28},{28,0},{1,5},{5... | collective-permute-start | bytes 786440 | tf_op jit(solution)/shard_map/ppermute | solution.py:21
  11.3 9.2 %collective-permute-start.7 = (bf16[512,256]{1,0:T(8,128)(2,1)S(1)}, bf16[512,256]{1,0:T(8,128)(2,1)S(1)}, u32[]{:S(2)}, u32[]{:S(2)}) collective-permute-start(bf16[512,256]{1,0:T(8,128)(2,1)S(1)} %part.13), channel_id=1, source_target_pairs={{0,1},{1,2},{2,3},{3,0},{4,5},{5,6},{6,7},{7,4},{8,9},{9,10},{10,1... | collective-permute-start | bytes 786440 | tf_op jit(solution)/shard_map/ppermute | solution.py:21
  15.5 11.2 %collective-permute-start.2 = (bf16[512,256]{1,0:T(8,128)(2,1)S(1)}, bf16[512,256]{1,0:T(8,128)(2,1)S(1)}, u32[]{:S(2)}, u32[]{:S(2)}) collective-permute-start(bf16[512,256]{1,0:T(8,128)(2,1)S(1)} %part.9), channel_id=1, source_target_pairs={{0,4},{4,8},{8,12},{12,16},{16,20},{20,24},{24,28},{28,0},{1,5},{5... | collective-permute-start | bytes 786440 | tf_op jit(solution)/shard_map/ppermute | solution.py:21
  16.0 10.7 %collective-permute-start.3 = (bf16[512,256]{1,0:T(8,128)(2,1)S(1)}, bf16[512,256]{1,0:T(8,128)(2,1)S(1)}, u32[]{:S(2)}, u32[]{:S(2)}) collective-permute-start(bf16[512,256]{1,0:T(8,128)(2,1)S(1)} %part.10), channel_id=1, source_target_pairs={{0,1},{1,2},{2,3},{3,0},{4,5},{5,6},{6,7},{7,4},{8,9},{9,10},{10,1... | collective-permute-start | bytes 786440 | tf_op jit(solution)/shard_map/ppermute | solution.py:21
  20.9 11.9 %collective-permute-start.8 = (bf16[512,256]{1,0:T(8,128)(2,1)S(1)}, bf16[512,256]{1,0:T(8,128)(2,1)S(1)}, u32[]{:S(2)}, u32[]{:S(2)}) collective-permute-start(bf16[512,256]{1,0:T(8,128)(2,1)S(1)} %part.14), channel_id=1, source_target_pairs={{0,4},{4,8},{8,12},{12,16},{16,20},{20,24},{24,28},{28,0},{1,5},{5... | collective-permute-start | bytes 786440 | tf_op jit(solution)/shard_map/ppermute | solution.py:21
  21.4 11.3 %collective-permute-start.9 = (bf16[512,256]{1,0:T(8,128)(2,1)S(1)}, bf16[512,256]{1,0:T(8,128)(2,1)S(1)}, u32[]{:S(2)}, u32[]{:S(2)}) collective-permute-start(bf16[512,256]{1,0:T(8,128)(2,1)S(1)} %part.15), channel_id=1, source_target_pairs={{0,1},{1,2},{2,3},{3,0},{4,5},{5,6},{6,7},{7,4},{8,9},{9,10},{10,1... | collective-permute-start | bytes 786440 | tf_op jit(solution)/shard_map/ppermute | solution.py:21
  27.2 10.8 %collective-permute-start.4 = (bf16[512,256]{1,0:T(8,128)(2,1)S(1)}, bf16[512,256]{1,0:T(8,128)(2,1)S(1)}, u32[]{:S(2)}, u32[]{:S(2)}) collective-permute-start(bf16[512,256]{1,0:T(8,128)(2,1)S(1)} %part.11), channel_id=1, source_target_pairs={{0,4},{4,8},{8,12},{12,16},{16,20},{20,24},{24,28},{28,0},{1,5},{5... | collective-permute-start | bytes 786440 | tf_op jit(solution)/shard_map/ppermute | solution.py:21
  27.7 7.3 %copy-start.1 = (s32[16,16]{1,0:T(8,128)S(1)}, s32[16,16]{1,0:T(8,128)}, u32[]{:S(2)}) copy-start(s32[16,16]{1,0:T(8,128)} %kinds.1) | copy-start | bytes 3076
  27.7 7.3 %copy-start.2 = (f32[16]{0:T(128)S(1)}, f32[16]{0:T(128)}, u32[]{:S(2)}) copy-start(f32[16]{0:T(128)} %table.1) | copy-start | bytes 196
  27.7 10.3 %copy-start = (bf16[1,1,256,1024]{3,2,1,0:T(8,128)(2,1)S(1)}, bf16[1,1,256,1024]{3,2,1,0:T(8,128)(2,1)}, u32[]{:S(2)}) copy-start(bf16[1,1,256,1024]{3,2,1,0:T(8,128)(2,1)} %param.7) | copy-start | bytes 1572868
  27.8 10.2 %collective-permute-start.5 = (bf16[512,256]{1,0:T(8,128)(2,1)S(1)}, bf16[512,256]{1,0:T(8,128)(2,1)S(1)}, u32[]{:S(2)}, u32[]{:S(2)}) collective-permute-start(bf16[512,256]{1,0:T(8,128)(2,1)S(1)} %part.12), channel_id=1, source_target_pairs={{0,1},{1,2},{2,3},{3,0},{4,5},{5,6},{6,7},{7,4},{8,9},{9,10},{10,1... | collective-permute-start | bytes 786440 | tf_op jit(solution)/shard_map/ppermute | solution.py:21
  33.2 6.7 %collective-permute-start.10 = (bf16[512,256]{1,0:T(8,128)(2,1)S(1)}, bf16[512,256]{1,0:T(8,128)(2,1)S(1)}, u32[]{:S(2)}, u32[]{:S(2)}) collective-permute-start(bf16[512,256]{1,0:T(8,128)(2,1)S(1)} %part.16), channel_id=1, source_target_pairs={{0,4},{4,8},{8,12},{12,16},{16,20},{20,24},{24,28},{1,5},{5,9},{9,... | collective-permute-start | bytes 786440 | tf_op jit(solution)/shard_map/ppermute | solution.py:26
  35.0 5.8 %collective-permute-start.11 = (bf16[512,256]{1,0:T(8,128)(2,1)S(1)}, bf16[512,256]{1,0:T(8,128)(2,1)S(1)}, u32[]{:S(2)}, u32[]{:S(2)}) collective-permute-start(bf16[512,256]{1,0:T(8,128)(2,1)S(1)} %part.17), channel_id=1, source_target_pairs={{0,1},{1,2},{2,3},{3,0},{4,5},{5,6},{6,7},{7,4},{8,9},{9,10},{10,1... | collective-permute-start | bytes 786440 | tf_op jit(solution)/shard_map/ppermute | solution.py:21
  41.1 4.5 %collective-permute-start.12 = (bf16[16,512]{1,0:T(8,128)(2,1)S(1)}, bf16[16,512]{1,0:T(8,128)(2,1)S(1)}, u32[]{:S(2)}, u32[]{:S(2)}) collective-permute-start(bf16[16,512]{1,0:T(8,128)(2,1)S(1)} %get-tuple-element.54), channel_id=1, source_target_pairs={{0,4},{1,5},{2,6},{3,7},{4,0},{5,1},{6,2},{7,3},{8,12},{9,13},{10,... | collective-permute-start | bytes 49160 | tf_op jit(solution)/shard_map/ppermute | solution.py:44
  42.7 2.8 %collective-permute-start.13 = (bf16[16,512]{1,0:T(8,128)(2,1)S(1)}, bf16[16,512]{1,0:T(8,128)(2,1)S(1)}, u32[]{:S(2)}, u32[]{:S(2)}) collective-permute-start(bf16[16,512]{1,0:T(8,128)(2,1)S(1)} %get-tuple-element.55), channel_id=1, source_target_pairs={{0,1},{1,0},{2,3},{3,2},{4,8},{5,9},{6,10},{7,11},{8,4},{9,5},{10,... | collective-permute-start | bytes 49160 | tf_op jit(solution)/shard_map/ppermute | solution.py:44
  42.8 2.8 %collective-permute-start.14 = (bf16[16,512]{1,0:T(8,128)(2,1)S(1)}, bf16[16,512]{1,0:T(8,128)(2,1)S(1)}, u32[]{:S(2)}, u32[]{:S(2)}) collective-permute-start(bf16[16,512]{1,0:T(8,128)(2,1)S(1)} %get-tuple-element.56), channel_id=1, source_target_pairs={{0,1},{1,0},{2,3},{3,2},{4,5},{5,4},{6,7},{7,6},{8,9},{9,8},{10,11... | collective-permute-start | bytes 49160 | tf_op jit(solution)/shard_map/ppermute | solution.py:44
  43.3 3.2 %collective-permute-start.15 = (bf16[16,512]{1,0:T(8,128)(2,1)S(1)}, bf16[16,512]{1,0:T(8,128)(2,1)S(1)}, u32[]{:S(2)}, u32[]{:S(2)}) collective-permute-start(bf16[16,512]{1,0:T(8,128)(2,1)S(1)} %get-tuple-element.57), channel_id=1, source_target_pairs={{0,3},{1,2},{2,1},{3,0},{4,7},{5,6},{6,5},{7,4},{8,11},{9,10},{10,... | collective-permute-start | bytes 49160 | tf_op jit(solution)/shard_map/ppermute | solution.py:44

commit v2 on v1

--- a/solution.py
+++ b/solution.py
@@ -98,7 +98,7 @@
         out_specs=(VMEM,) * 4,
         scratch_shapes=[pltpu.SemaphoreType.DMA((4,))],
         cost_estimate=cost(4 * trace * trace * width, 4 * trace * trace + 6 * trace * width),
-        compiler_params=PACKED,
+        compiler_params=PARAMS,
         name="first_right",
     )(z, left, lower)
 
@@ -150,7 +150,7 @@
         in_specs=[VMEM] * 3,
         out_specs=VMEM,
         cost_estimate=cost(4 * trace * trace * width, 4 * trace * trace + 6 * trace * width),
-        compiler_params=PACKED,
+        compiler_params=PARAMS,
         name="part",
     )(z, left, lower)
 
@@ -178,7 +178,7 @@
         out_specs=(VMEM,) * 3,
         scratch_shapes=[pltpu.SemaphoreType.DMA((2,))],
         cost_estimate=cost(4 * trace * trace * width, 4 * trace * trace + 6 * trace * width),
-        compiler_params=PACKED,
+        compiler_params=PARAMS,
         name="part_loading",
     )(z, left, lower)
 
@@ -269,7 +269,7 @@
         in_specs=[VMEM] * 4,
         out_specs=(VMEM,) * 4,
         cost_estimate=cost(2 * weights.size * width, 2 * weights.size + 4 * weights.shape[1] * width),
-        compiler_params=PACKED,
+        compiler_params=PARAMS,
         name="edges",
     )(weights, left, lower, done)
 
@@ -304,7 +304,7 @@
             pltpu.SemaphoreType.DMA((4,)),
         ],
         cost_estimate=cost(8 * trace * trace * width, 8 * trace * trace + 8 * trace * width),
-        compiler_params=PACKED,
+        compiler_params=PARAMS,
         name="last",
     )(z_top, z_low, left, lower)
 
@@ -411,7 +411,7 @@
 
 
 def finish(inner, upper, halos, before):
-    groups = 2 if inner.shape[0] % 2 == 0 else 1
+    groups = 1
     given = 2 + len(halos)
     return pl.pallas_call(
         finish_kernel,

time: 47.6 us -> 47.6 us (level)
  no operation moved by 1% of the time
where the time goes in v2:
time: 47.6 us; the launch traced here: 47.3 us
  waiting for transfers between devices  20.7 us (43%)
  Pallas kernels  14.3 us (30%)
  starting transfers between devices  11.4 us (24%)
  between operations  0.89 us (2%)
    ppermute x11, waiting for transfers between devices, around(): lax.ppermute(block, axis, [(i, (i + 1) % count) for i in range(count)])  19.7 us
    ppermute x11, starting transfers between devices, around(): lax.ppermute(block, axis, [(i, (i + 1) % count) for i in range(count)])  6.93 us
    pallas_call x9, Pallas kernels, part(): pl.pallas_call(functools.partial(part_kernel, axis), out_shape=jax.ShapeD...  3.92 us
    ppermute x4, starting transfers between devices, swapped(): return lax.ppermute(block, names, pairs)  3.13 us
    pallas_call x1, Pallas kernels, first_right(): pl.pallas_call(functools.partial(first_right_kernel, base, width), out_sh...  2.08 us
    pallas_call x1, Pallas kernels, first_upper(): pl.pallas_call(first_upper_kernel, out_shape=(vmem(trace, width), vmem(tr...  1.9 us
    pallas_call x1, Pallas kernels, part_loading(): pl.pallas_call(functools.partial(part_loading_kernel, axis, base), out_sh...  1.49 us
    pallas_call x1, Pallas kernels, last(): pl.pallas_call(last_kernel, out_shape=(out, out), in_specs=[VMEM] * 4, ou...  1.45 us
  transfers between devices with their start and end apart: 16, of which 8 were waited for; matrix products, arithmetic and copies ran while one was open for 0% of the time, Pallas kernels for 24%

profile of v2, /device:TPU:0, one launch (start us, length us, event | category | flops | bytes accessed | tf_op | source)
XLA Modules:
  0.0 47.3 jit_solution(1192423577487539067)
XLA Ops:
  0.6 2.1 %first_right.1 = (bf16[512,256]{1,0:T(8,128)(2,1)S(1)}, bf16[512,1024]{1,0:T(8,128)(2,1)S(1)}, bf16[512,256]{1,0:T(8,128)(2,1)S(1)}, bf16[512,256]{1,0:T(8,128)(2,1)S(1)}) custom-call(bf16[1024,1024]{1,0:T(8,128)(2,1)} %bitcast.8, bf16[512,512]{1,0:T(8,128)(2,1)} %bitcast.10, bf16[512,512]{1,0:T(8,128)(2,1)} %bitcast.12), custom_call_target="tpu_custom_call" | custom-call | flops 268435456 | bytes 1835008 | tf_op jit(solution)/shard_map/first_right/pallas_call | solution.py:94
  2.7 3.0 %collective-permute-start = (bf16[512,256]{1,0:T(8,128)(2,1)S(1)}, bf16[512,256]{1,0:T(8,128)(2,1)S(1)}, u32[]{:S(2)}, u32[]{:S(2)}) collective-permute-start(bf16[512,256]{1,0:T(8,128)(2,1)S(1)} %get-tuple-element.36), channel_id=1, source_target_pairs={{0,4},{4,8},{8,12},{12,16},{16,20},{20,24},{24,28},{28,0},{1,5},{5... | collective-permute-start | bytes 786440 | tf_op jit(solution)/shard_map/ppermute | solution.py:21
  5.7 1.9 %first_upper.1 = (bf16[512,256]{1,0:T(8,128)(2,1)S(1)}, bf16[512,1024]{1,0:T(8,128)(2,1)S(1)}) custom-call(bf16[1024,1024]{1,0:T(8,128)(2,1)} %bitcast.9, bf16[512,256]{1,0:T(8,128)(2,1)S(1)} %get-tuple-element.33.left, bf16[512,256]{1,0:T(8,128)(2,1)S(1)} %get-tuple-element.34.lower), custom_call_target="tpu_custom_call" | custom-call | flops 268435456 | bytes 1835008 | tf_op jit(solution)/shard_map/first_upper/pallas_call | solution.py:125
  7.6 0.1 collective-permute-start.1
  7.7 1.5 %part_loading.1 = (bf16[512,256]{1,0:T(8,128)(2,1)S(1)}, bf16[512,256]{1,0:T(8,128)(2,1)S(1)}, bf16[512,256]{1,0:T(8,128)(2,1)S(1)}) custom-call(bf16[512,1024]{1,0:T(8,128)(2,1)S(1)} %get-tuple-element.32.z.z_top, bf16[512,512]{1,0:T(8,128)(2,1)} %bitcast.11, bf16[512,512]{1,0:T(8,128)(2,1)} %bitcast.13), custom_call_target="tpu_custom_call" | custom-call | flops 268435456 | bytes 1835008 | tf_op jit(solution)/shard_map/part_loading/pallas_call | solution.py:174
  9.2 1.6 %collective-permute-start.6 = (bf16[512,256]{1,0:T(8,128)(2,1)S(1)}, bf16[512,256]{1,0:T(8,128)(2,1)S(1)}, u32[]{:S(2)}, u32[]{:S(2)}) collective-permute-start(bf16[512,256]{1,0:T(8,128)(2,1)S(1)} %get-tuple-element.39), channel_id=1, source_target_pairs={{0,4},{4,8},{8,12},{12,16},{16,20},{20,24},{24,28},{28,0},{1,5},{5... | collective-permute-start | bytes 786440 | tf_op jit(solution)/shard_map/ppermute | solution.py:21
  10.8 0.4 part.13
  11.3 1.4 %collective-permute-start.7 = (bf16[512,256]{1,0:T(8,128)(2,1)S(1)}, bf16[512,256]{1,0:T(8,128)(2,1)S(1)}, u32[]{:S(2)}, u32[]{:S(2)}) collective-permute-start(bf16[512,256]{1,0:T(8,128)(2,1)S(1)} %part.13), channel_id=1, source_target_pairs={{0,1},{1,2},{2,3},{3,0},{4,5},{5,6},{6,7},{7,4},{8,9},{9,10},{10,1... | collective-permute-start | bytes 786440 | tf_op jit(solution)/shard_map/ppermute | solution.py:21
  12.6 2.4 %collective-permute-done.left = bf16[512,256]{1,0:T(8,128)(2,1)S(1)} collective-permute-done((bf16[512,256]{1,0:T(8,128)(2,1)S(1)}, bf16[512,256]{1,0:T(8,128)(2,1)S(1)}, u32[]{:S(2)}, u32[]{:S(2)}) %collective-permute-start) | collective-permute-done | bytes 262176 | tf_op jit(solution)/shard_map/ppermute | solution.py:21
  15.1 0.0 collective-permute-done.1.lower
  15.1 0.4 part.9
  15.5 0.1 collective-permute-start.2
  15.6 0.4 part.10
  16.0 0.1 collective-permute-start.3
  16.1 4.4 %collective-permute-done.6.left = bf16[512,256]{1,0:T(8,128)(2,1)S(1)} collective-permute-done((bf16[512,256]{1,0:T(8,128)(2,1)S(1)}, bf16[512,256]{1,0:T(8,128)(2,1)S(1)}, u32[]{:S(2)}, u32[]{:S(2)}) %collective-permute-start.6) | collective-permute-done | bytes 262176 | tf_op jit(solution)/shard_map/ppermute | solution.py:21
  20.5 0.0 collective-permute-done.7.lower
  20.5 0.4 part.14
  20.9 0.1 collective-permute-start.8
  21.0 0.4 part.15
  21.4 0.5 %collective-permute-start.9 = (bf16[512,256]{1,0:T(8,128)(2,1)S(1)}, bf16[512,256]{1,0:T(8,128)(2,1)S(1)}, u32[]{:S(2)}, u32[]{:S(2)}) collective-permute-start(bf16[512,256]{1,0:T(8,128)(2,1)S(1)} %part.15), channel_id=1, source_target_pairs={{0,1},{1,2},{2,3},{3,0},{4,5},{5,6},{6,7},{7,4},{8,9},{9,10},{10,1... | collective-permute-start | bytes 786440 | tf_op jit(solution)/shard_map/ppermute | solution.py:21
  22.0 4.8 %collective-permute-done.2.left = bf16[512,256]{1,0:T(8,128)(2,1)S(1)} collective-permute-done((bf16[512,256]{1,0:T(8,128)(2,1)S(1)}, bf16[512,256]{1,0:T(8,128)(2,1)S(1)}, u32[]{:S(2)}, u32[]{:S(2)}) %collective-permute-start.2) | collective-permute-done | bytes 262176 | tf_op jit(solution)/shard_map/ppermute | solution.py:21
  26.8 0.0 collective-permute-done.3.lower
  26.8 0.4 part.11
  27.2 0.1 collective-permute-start.4
  27.3 0.4 part.12
  27.7 0.0 copy-start.1
  27.7 0.0 copy-start.2
  27.7 0.0 copy-start
  27.8 0.1 collective-permute-start.5
  27.8 5.0 %collective-permute-done.8.left = bf16[512,256]{1,0:T(8,128)(2,1)S(1)} collective-permute-done((bf16[512,256]{1,0:T(8,128)(2,1)S(1)}, bf16[512,256]{1,0:T(8,128)(2,1)S(1)}, u32[]{:S(2)}, u32[]{:S(2)}) %collective-permute-start.8) | collective-permute-done | bytes 262176 | tf_op jit(solution)/shard_map/ppermute | solution.py:21
  32.8 0.0 collective-permute-done.9.lower
  32.8 0.4 part.16
  33.2 1.3 %collective-permute-start.10 = (bf16[512,256]{1,0:T(8,128)(2,1)S(1)}, bf16[512,256]{1,0:T(8,128)(2,1)S(1)}, u32[]{:S(2)}, u32[]{:S(2)}) collective-permute-start(bf16[512,256]{1,0:T(8,128)(2,1)S(1)} %part.16), channel_id=1, source_target_pairs={{0,4},{4,8},{8,12},{12,16},{16,20},{20,24},{24,28},{1,5},{5,9},{9,... | collective-permute-start | bytes 786440 | tf_op jit(solution)/shard_map/ppermute | solution.py:26
  34.6 0.4 part.17
  35.0 0.1 collective-permute-start.11
  35.1 0.0 copy-done.1
  35.1 0.0 copy-done.2
  35.1 0.7 %wavenum.1 = f32[256,128]{1,0:T(8,128)S(1)} custom-call(f32[16]{0:T(128)S(1)} %copy-done.2, s32[16,16]{1,0:T(8,128)S(1)} %copy-done.1), custom_call_target="tpu_custom_call" | custom-call | tf_op jit(solution)/shard_map/wavenum/pallas_call | solution.py:200
  35.7 2.3 %collective-permute-done.4.left = bf16[512,256]{1,0:T(8,128)(2,1)S(1)} collective-permute-done((bf16[512,256]{1,0:T(8,128)(2,1)S(1)}, bf16[512,256]{1,0:T(8,128)(2,1)S(1)}, u32[]{:S(2)}, u32[]{:S(2)}) %collective-permute-start.4) | collective-permute-done | bytes 262176 | tf_op jit(solution)/shard_map/ppermute | solution.py:21
  38.0 0.0 collective-permute-done.5.lower
  38.0 0.0 copy-done
  38.0 0.4 volume.1
  38.4 1.4 %last.1 = (bf16[512,512]{1,0:T(8,128)(2,1)}, bf16[512,512]{1,0:T(8,128)(2,1)}) custom-call(bf16[512,1024]{1,0:T(8,128)(2,1)S(1)} %get-tuple-element.32.z.z_top, bf16[512,1024]{1,0:T(8,128)(2,1)S(1)} %get-tuple-element.35.z.z_low, bf16[512,256]{1,0:T(8,128)(2,1)S(1)} %collective-permute-done.4.left, bf16[512,256]{1,0:T(8,128)(2,1)S(1)} %collective-permute-done.5.lower), custom_call_target="tpu_custom_call" | custom-call | flops 536870912 | bytes 3145728 | tf_op jit(solution)/shard_map/last/pallas_call | solution.py:296
  39.8 0.2 collective-permute-done.10.left
  40.0 0.9 %collective-permute-done.11.lower = bf16[512,256]{1,0:T(8,128)(2,1)S(1)} collective-permute-done((bf16[512,256]{1,0:T(8,128)(2,1)S(1)}, bf16[512,256]{1,0:T(8,128)(2,1)S(1)}, u32[]{:S(2)}, u32[]{:S(2)}) %collective-permute-start.11) | collective-permute-done | bytes 262176 | tf_op jit(solution)/shard_map/ppermute | solution.py:21
  40.8 0.2 edges.1
  41.1 1.7 %collective-permute-start.12 = (bf16[16,512]{1,0:T(8,128)(2,1)S(1)}, bf16[16,512]{1,0:T(8,128)(2,1)S(1)}, u32[]{:S(2)}, u32[]{:S(2)}) collective-permute-start(bf16[16,512]{1,0:T(8,128)(2,1)S(1)} %get-tuple-element.54), channel_id=1, source_target_pairs={{0,4},{1,5},{2,6},{3,7},{4,0},{5,1},{6,2},{7,3},{8,12},{9,13},{10,... | collective-permute-start | bytes 49160 | tf_op jit(solution)/shard_map/ppermute | solution.py:44
  42.7 0.0 collective-permute-start.13
  42.8 0.5 %collective-permute-start.14 = (bf16[16,512]{1,0:T(8,128)(2,1)S(1)}, bf16[16,512]{1,0:T(8,128)(2,1)S(1)}, u32[]{:S(2)}, u32[]{:S(2)}) collective-permute-start(bf16[16,512]{1,0:T(8,128)(2,1)S(1)} %get-tuple-element.56), channel_id=1, source_target_pairs={{0,1},{1,0},{2,3},{3,2},{4,5},{5,4},{6,7},{7,6},{8,9},{9,8},{10,11... | collective-permute-start | bytes 49160 | tf_op jit(solution)/shard_map/ppermute | solution.py:44
  43.3 0.9 %collective-permute-start.15 = (bf16[16,512]{1,0:T(8,128)(2,1)S(1)}, bf16[16,512]{1,0:T(8,128)(2,1)S(1)}, u32[]{:S(2)}, u32[]{:S(2)}) collective-permute-start(bf16[16,512]{1,0:T(8,128)(2,1)S(1)} %get-tuple-element.57), channel_id=1, source_target_pairs={{0,3},{1,2},{2,1},{3,0},{4,7},{5,6},{6,5},{7,4},{8,11},{9,10},{10,... | collective-permute-start | bytes 49160 | tf_op jit(solution)/shard_map/ppermute | solution.py:44
  44.2 1.4 %plain.1 = (bf16[512,512]{1,0:T(8,128)(2,1)}, f32[16,16,512]{2,1,0:T(8,128)S(1)}, bf16[512,256]{1,0:T(8,128)(2,1)S(1)}) custom-call(bf16[512,1024]{1,0:T(8,128)(2,1)S(1)} %get-tuple-element.32.z.z_top, bf16[512,1024]{1,0:T(8,128)(2,1)S(1)} %get-tuple-element.35.z.z_low, bf16[256,1024]{1,0:T(8,128)(2,1)S(1)} %bitcast.7, ...), custom_call_target="tpu_custom_call", output_to_operand_aliasing={{0}: (7, {})} | custom-call | flops 536870912 | bytes 3145728 | tf_op jit(solution)/shard_map/plain/pallas_call | solution.py:354
  45.6 0.0 collective-permute-done.12.x_pair
  45.6 0.0 collective-permute-done.13.x_cross
  45.6 0.0 collective-permute-done.14.y_pair
  45.6 0.8 %collective-permute-done.15.y_cross = bf16[16,512]{1,0:T(8,128)(2,1)S(1)} collective-permute-done((bf16[16,512]{1,0:T(8,128)(2,1)S(1)}, bf16[16,512]{1,0:T(8,128)(2,1)S(1)}, u32[]{:S(2)}, u32[]{:S(2)}) %collective-permute-start.15) | collective-permute-done | bytes 16416 | tf_op jit(solution)/shard_map/ppermute | solution.py:44
  46.4 0.9 %finish.1 = (bf16[512,512]{1,0:T(8,128)(2,1)}, f32[16,16,512]{2,1,0:T(8,128)}) custom-call(f32[16,16,512]{2,1,0:T(8,128)S(1)} %get-tuple-element.50.inner, bf16[512,256]{1,0:T(8,128)(2,1)S(1)} %get-tuple-element.51.upper, bf16[16,512]{1,0:T(8,128)(2,1)S(1)} %collective-permute-done.12.x_pair, ...), custom_call_target="tpu_custom_call", output_to_operand_aliasing={{0}: (6, {})} | custom-call | flops 524288 | bytes 1048576 | tf_op jit(solution)/shard_map/finish/pallas_call | solution.py:416
Async XLA Ops:
  2.7 12.4 %collective-permute-start = (bf16[512,256]{1,0:T(8,128)(2,1)S(1)}, bf16[512,256]{1,0:T(8,128)(2,1)S(1)}, u32[]{:S(2)}, u32[]{:S(2)}) collective-permute-start(bf16[512,256]{1,0:T(8,128)(2,1)S(1)} %get-tuple-element.36), channel_id=1, source_target_pairs={{0,4},{4,8},{8,12},{12,16},{16,20},{20,24},{24,28},{28,0},{1,5},{5... | collective-permute-start | bytes 786440 | tf_op jit(solution)/shard_map/ppermute | solution.py:21
  7.6 7.4 %collective-permute-start.1 = (bf16[512,256]{1,0:T(8,128)(2,1)S(1)}, bf16[512,256]{1,0:T(8,128)(2,1)S(1)}, u32[]{:S(2)}, u32[]{:S(2)}) collective-permute-start(bf16[512,256]{1,0:T(8,128)(2,1)S(1)} %get-tuple-element.37), channel_id=1, source_target_pairs={{0,1},{1,2},{2,3},{3,0},{4,5},{5,6},{6,7},{7,4},{8,9},{9,10},{10,1... | collective-permute-start | bytes 786440 | tf_op jit(solution)/shard_map/ppermute | solution.py:21
  9.2 11.3 %collective-permute-start.6 = (bf16[512,256]{1,0:T(8,128)(2,1)S(1)}, bf16[512,256]{1,0:T(8,128)(2,1)S(1)}, u32[]{:S(2)}, u32[]{:S(2)}) collective-permute-start(bf16[512,256]{1,0:T(8,128)(2,1)S(1)} %get-tuple-element.39), channel_id=1, source_target_pairs={{0,4},{4,8},{8,12},{12,16},{16,20},{20,24},{24,28},{28,0},{1,5},{5... | collective-permute-start | bytes 786440 | tf_op jit(solution)/shard_map/ppermute | solution.py:21
  11.3 9.2 %collective-permute-start.7 = (bf16[512,256]{1,0:T(8,128)(2,1)S(1)}, bf16[512,256]{1,0:T(8,128)(2,1)S(1)}, u32[]{:S(2)}, u32[]{:S(2)}) collective-permute-start(bf16[512,256]{1,0:T(8,128)(2,1)S(1)} %part.13), channel_id=1, source_target_pairs={{0,1},{1,2},{2,3},{3,0},{4,5},{5,6},{6,7},{7,4},{8,9},{9,10},{10,1... | collective-permute-start | bytes 786440 | tf_op jit(solution)/shard_map/ppermute | solution.py:21
  15.5 11.2 %collective-permute-start.2 = (bf16[512,256]{1,0:T(8,128)(2,1)S(1)}, bf16[512,256]{1,0:T(8,128)(2,1)S(1)}, u32[]{:S(2)}, u32[]{:S(2)}) collective-permute-start(bf16[512,256]{1,0:T(8,128)(2,1)S(1)} %part.9), channel_id=1, source_target_pairs={{0,4},{4,8},{8,12},{12,16},{16,20},{20,24},{24,28},{28,0},{1,5},{5... | collective-permute-start | bytes 786440 | tf_op jit(solution)/shard_map/ppermute | solution.py:21
  16.0 10.7 %collective-permute-start.3 = (bf16[512,256]{1,0:T(8,128)(2,1)S(1)}, bf16[512,256]{1,0:T(8,128)(2,1)S(1)}, u32[]{:S(2)}, u32[]{:S(2)}) collective-permute-start(bf16[512,256]{1,0:T(8,128)(2,1)S(1)} %part.10), channel_id=1, source_target_pairs={{0,1},{1,2},{2,3},{3,0},{4,5},{5,6},{6,7},{7,4},{8,9},{9,10},{10,1... | collective-permute-start | bytes 786440 | tf_op jit(solution)/shard_map/ppermute | solution.py:21
  20.9 11.9 %collective-permute-start.8 = (bf16[512,256]{1,0:T(8,128)(2,1)S(1)}, bf16[512,256]{1,0:T(8,128)(2,1)S(1)}, u32[]{:S(2)}, u32[]{:S(2)}) collective-permute-start(bf16[512,256]{1,0:T(8,128)(2,1)S(1)} %part.14), channel_id=1, source_target_pairs={{0,4},{4,8},{8,12},{12,16},{16,20},{20,24},{24,28},{28,0},{1,5},{5... | collective-permute-start | bytes 786440 | tf_op jit(solution)/shard_map/ppermute | solution.py:21
  21.4 11.3 %collective-permute-start.9 = (bf16[512,256]{1,0:T(8,128)(2,1)S(1)}, bf16[512,256]{1,0:T(8,128)(2,1)S(1)}, u32[]{:S(2)}, u32[]{:S(2)}) collective-permute-start(bf16[512,256]{1,0:T(8,128)(2,1)S(1)} %part.15), channel_id=1, source_target_pairs={{0,1},{1,2},{2,3},{3,0},{4,5},{5,6},{6,7},{7,4},{8,9},{9,10},{10,1... | collective-permute-start | bytes 786440 | tf_op jit(solution)/shard_map/ppermute | solution.py:21
  27.2 10.8 %collective-permute-start.4 = (bf16[512,256]{1,0:T(8,128)(2,1)S(1)}, bf16[512,256]{1,0:T(8,128)(2,1)S(1)}, u32[]{:S(2)}, u32[]{:S(2)}) collective-permute-start(bf16[512,256]{1,0:T(8,128)(2,1)S(1)} %part.11), channel_id=1, source_target_pairs={{0,4},{4,8},{8,12},{12,16},{16,20},{20,24},{24,28},{28,0},{1,5},{5... | collective-permute-start | bytes 786440 | tf_op jit(solution)/shard_map/ppermute | solution.py:21
  27.7 7.3 %copy-start.1 = (s32[16,16]{1,0:T(8,128)S(1)}, s32[16,16]{1,0:T(8,128)}, u32[]{:S(2)}) copy-start(s32[16,16]{1,0:T(8,128)} %kinds.1) | copy-start | bytes 3076
  27.7 7.3 %copy-start.2 = (f32[16]{0:T(128)S(1)}, f32[16]{0:T(128)}, u32[]{:S(2)}) copy-start(f32[16]{0:T(128)} %table.1) | copy-start | bytes 196
  27.7 10.3 %copy-start = (bf16[1,1,256,1024]{3,2,1,0:T(8,128)(2,1)S(1)}, bf16[1,1,256,1024]{3,2,1,0:T(8,128)(2,1)}, u32[]{:S(2)}) copy-start(bf16[1,1,256,1024]{3,2,1,0:T(8,128)(2,1)} %param.7) | copy-start | bytes 1572868
  27.8 10.2 %collective-permute-start.5 = (bf16[512,256]{1,0:T(8,128)(2,1)S(1)}, bf16[512,256]{1,0:T(8,128)(2,1)S(1)}, u32[]{:S(2)}, u32[]{:S(2)}) collective-permute-start(bf16[512,256]{1,0:T(8,128)(2,1)S(1)} %part.12), channel_id=1, source_target_pairs={{0,1},{1,2},{2,3},{3,0},{4,5},{5,6},{6,7},{7,4},{8,9},{9,10},{10,1... | collective-permute-start | bytes 786440 | tf_op jit(solution)/shard_map/ppermute | solution.py:21
  33.2 6.7 %collective-permute-start.10 = (bf16[512,256]{1,0:T(8,128)(2,1)S(1)}, bf16[512,256]{1,0:T(8,128)(2,1)S(1)}, u32[]{:S(2)}, u32[]{:S(2)}) collective-permute-start(bf16[512,256]{1,0:T(8,128)(2,1)S(1)} %part.16), channel_id=1, source_target_pairs={{0,4},{4,8},{8,12},{12,16},{16,20},{20,24},{24,28},{1,5},{5,9},{9,... | collective-permute-start | bytes 786440 | tf_op jit(solution)/shard_map/ppermute | solution.py:26
  35.0 5.8 %collective-permute-start.11 = (bf16[512,256]{1,0:T(8,128)(2,1)S(1)}, bf16[512,256]{1,0:T(8,128)(2,1)S(1)}, u32[]{:S(2)}, u32[]{:S(2)}) collective-permute-start(bf16[512,256]{1,0:T(8,128)(2,1)S(1)} %part.17), channel_id=1, source_target_pairs={{0,1},{1,2},{2,3},{3,0},{4,5},{5,6},{6,7},{7,4},{8,9},{9,10},{10,1... | collective-permute-start | bytes 786440 | tf_op jit(solution)/shard_map/ppermute | solution.py:21
  41.1 4.5 %collective-permute-start.12 = (bf16[16,512]{1,0:T(8,128)(2,1)S(1)}, bf16[16,512]{1,0:T(8,128)(2,1)S(1)}, u32[]{:S(2)}, u32[]{:S(2)}) collective-permute-start(bf16[16,512]{1,0:T(8,128)(2,1)S(1)} %get-tuple-element.54), channel_id=1, source_target_pairs={{0,4},{1,5},{2,6},{3,7},{4,0},{5,1},{6,2},{7,3},{8,12},{9,13},{10,... | collective-permute-start | bytes 49160 | tf_op jit(solution)/shard_map/ppermute | solution.py:44
  42.7 2.8 %collective-permute-start.13 = (bf16[16,512]{1,0:T(8,128)(2,1)S(1)}, bf16[16,512]{1,0:T(8,128)(2,1)S(1)}, u32[]{:S(2)}, u32[]{:S(2)}) collective-permute-start(bf16[16,512]{1,0:T(8,128)(2,1)S(1)} %get-tuple-element.55), channel_id=1, source_target_pairs={{0,1},{1,0},{2,3},{3,2},{4,8},{5,9},{6,10},{7,11},{8,4},{9,5},{10,... | collective-permute-start | bytes 49160 | tf_op jit(solution)/shard_map/ppermute | solution.py:44
  42.8 2.8 %collective-permute-start.14 = (bf16[16,512]{1,0:T(8,128)(2,1)S(1)}, bf16[16,512]{1,0:T(8,128)(2,1)S(1)}, u32[]{:S(2)}, u32[]{:S(2)}) collective-permute-start(bf16[16,512]{1,0:T(8,128)(2,1)S(1)} %get-tuple-element.56), channel_id=1, source_target_pairs={{0,1},{1,0},{2,3},{3,2},{4,5},{5,4},{6,7},{7,6},{8,9},{9,8},{10,11... | collective-permute-start | bytes 49160 | tf_op jit(solution)/shard_map/ppermute | solution.py:44
  43.3 3.2 %collective-permute-start.15 = (bf16[16,512]{1,0:T(8,128)(2,1)S(1)}, bf16[16,512]{1,0:T(8,128)(2,1)S(1)}, u32[]{:S(2)}, u32[]{:S(2)}) collective-permute-start(bf16[16,512]{1,0:T(8,128)(2,1)S(1)} %get-tuple-element.57), channel_id=1, source_target_pairs={{0,3},{1,2},{2,1},{3,0},{4,7},{5,6},{6,5},{7,4},{8,11},{9,10},{10,... | collective-permute-start | bytes 49160 | tf_op jit(solution)/shard_map/ppermute | solution.py:44
